TPU v7x, 128 devices: a whole 4x4x4 slice. The times are simulated.
128 devices in a mesh: flow: 16 (over x, z), cross: 8 (over y, core).
Axes of the slice: x: 4, y: 4, z: 4, core: 2. Of those that a mesh axis runs over, the one named last changes fastest.
Arguments:
- right_side: float32 [16, 512, 320], P('flow', 'cross'), may hold values from -6 to 6
- old_state: float32 [16, 512, 320], P('flow', 'cross'), may hold values from -6 to 6
- block_inverse: bfloat16 [16, 512, 320, 320], P('flow', 'cross'), as said below
- flux_jacobian: float32 [16, 512, 4, 25], P('flow', 'cross'), may hold values from -1.35 to 1.35, as said below
- face_lift: float32 [4, 64, 64], replicated, may hold values from -0.75 to 0.75
- upstream: int32 [16, 512], P('flow', 'cross'), may hold values from 0 to 511, as said below
- downstream: int32 [16, 512], P('flow', 'cross'), may hold values from 0 to 511, as said below
- live_counts: int32 [16, 8], P('flow', 'cross'), may hold values from 32 to 64, as said below
Outputs:
- half_sweep: float32 [16, 512, 320], P('flow', 'cross')
- full_sweep: float32 [16, 512, 320], P('flow', 'cross')
Inputs may be any that keep to these rules, and one draw needn't show every extreme that they name: In each layer the upstream slots of an aligned block of 4 slots are a permutation of that same block's slots. downstream[l] is the inverse permutation of upstream[l + 1] (of upstream[0] for the last layer): upstream[l + 1, downstream[l, e]] = e. `live_counts`: slots at or beyond the count in their run hold no element; some run is full. `block_inverse`: each block is the sum of a multiple of the identity and a full dense part. `flux_jacobian`: entries are centred; those of the upstream and downstream faces are of order 0.45, those of the left and right faces of order 0.27.
All inputs are finite; a program needn't handle non-finite values.
Results may differ from a plain program's by a relative error of at most 0.017.
Values sent between devices are 32-bit elements; how exact they have to be, the bound alone decides.
No kernel may reach another device: no remote copies, remote signals or barrier semaphores. Data moves between devices by JAX's collectives and lax.ppermute only.
A program may use at most 64 MiB of HBM per device.

v0:
```python
import jax
import jax.numpy as jnp
from jax import lax
from jax.sharding import PartitionSpec as P

GRP = 4


HIGHEST_PRECISION = lax.Precision.HIGHEST


def passed_along(block, axis, distance):
    devices = range(lax.axis_size(axis))
    route = [(i - distance, i) for i in devices if i - distance in devices]
    return lax.ppermute(block, axis, route)


def extended(cells, sides, width):
    for axis, dim in sides:
        count = lax.axis_size(axis)
        ends = count - 1
        head = lax.slice_in_dim(cells, 0, width, axis=dim)
        tail = lax.slice_in_dim(cells, cells.shape[dim] - width, cells.shape[dim], axis=dim)
        cells = jnp.concatenate(
            [
                lax.ppermute(tail, axis, [(i, (i + 1) % count) for i in range(ends)]),
                cells,
                lax.ppermute(head, axis, [((i + 1) % count, i) for i in range(ends)]),
            ],
            axis=dim,
        )
    return cells


def couple(values, lift, jacobian_face):
    spread = jnp.einsum("...vc,bc->...vb", values, lift, precision=HIGHEST_PRECISION)
    mixing = jacobian_face.reshape(jacobian_face.shape[:-1] + (5, 5))
    return jnp.einsum("...uv,...vb->...ub", mixing, spread, precision=HIGHEST_PRECISION)


def solve_blocks(inverse, residual, live):
    flat = residual.reshape(residual.shape[:-2] + (-1,)).astype(jnp.bfloat16)
    solved = jnp.einsum("...ij,...j->...i", inverse, flat, preferred_element_type=jnp.float32)
    return (solved * live[..., None]).reshape(residual.shape)


def group_slices(start_elem, group_width, arrays):
    return [lax.dynamic_slice_in_dim(item, start_elem, group_width, 1) for item in arrays]


def forward_chain(fixed_fwd, block_inverse, jacobian_up, lift_up, up_local, live, group_count):
    layer_count, elem_count = up_local.shape
    group_width = elem_count // group_count
    flow_size = lax.axis_size("flow")
    flow_place = lax.axis_index("flow")
    block_shape = (layer_count, group_width) + fixed_fwd.shape[2:]

    def forward_run_group(inbound, start_elem):
        fixed_part, inverse_part, jacobian_part, index_part, live_part = group_slices(
            start_elem, group_width, (fixed_fwd, block_inverse, jacobian_up, up_local, live)
        )
        index_part = index_part - start_elem
        nearest = inbound[index_part[0]]
        solved = solve_blocks(
            inverse_part[0],
            fixed_part[0] - couple(nearest, lift_up, jacobian_part[0]),
            live_part[0],
        )
        solved_rows = [solved]
        return (jnp.stack(solved_rows), solved)

    def forward_skip_group(inbound, start_elem):
        return (jnp.zeros(block_shape, jnp.float32), jnp.zeros_like(inbound))

    def forward_run_section(step_index, carried):
        outbound, gathered, received = carried
        inbound = passed_along(outbound, "flow", 1)
        group_index = step_index - flow_place
        start_elem = jnp.clip(group_index, 0, group_count - 1) * group_width
        usable = (group_index >= 0) & (group_index < group_count)
        solved_block, last_layer = lax.cond(
            usable, forward_run_group, forward_skip_group, inbound, start_elem
        )
        updated = lax.dynamic_update_slice_in_dim(gathered, solved_block, start_elem, 1)
        stored = lax.dynamic_update_slice_in_dim(received, inbound, start_elem, 0)
        return (
            last_layer,
            jnp.where(usable, updated, gathered),
            jnp.where(usable, stored, received),
        )

    initial = (
        jnp.zeros((group_width,) + fixed_fwd.shape[2:], jnp.float32),
        jnp.zeros_like(fixed_fwd),
        jnp.zeros_like(fixed_fwd[0]),
    )
    _, result, received = lax.fori_loop(
        0, flow_size + group_count - 1, forward_run_section, initial
    )
    return (result, received)


def backward_chain(
    fixed_bwd, block_inverse, jacobian_down, lift_down, down_local, live, group_count
):
    layer_count, elem_count = down_local.shape
    group_width = elem_count // group_count
    flow_size = lax.axis_size("flow")
    flow_place = lax.axis_index("flow")
    block_shape = (layer_count, group_width) + fixed_bwd.shape[2:]

    def backward_run_group(inbound, start_elem):
        fixed_part, inverse_part, jacobian_part, index_part, live_part = group_slices(
            start_elem, group_width, (fixed_bwd, block_inverse, jacobian_down, down_local, live)
        )
        index_part = index_part - start_elem
        later = inbound
        solved_rows = [None] * layer_count
        for layer_pos in reversed(range(layer_count)):
            nearest = later[index_part[layer_pos]]
            solved = solve_blocks(
                inverse_part[layer_pos],
                fixed_part[layer_pos] - couple(nearest, lift_down, jacobian_part[layer_pos]),
                live_part[layer_pos],
            )
            solved_rows[layer_pos] = solved
            later = solved
        return (jnp.stack(solved_rows), later)

    def backward_skip_group(inbound, start_elem):
        return (jnp.zeros(block_shape, jnp.float32), jnp.zeros_like(inbound))

    def backward_run_section(step_index, carried):
        outbound, gathered = carried
        inbound = passed_along(outbound, "flow", -1)
        group_index = step_index - (flow_size - 1 - flow_place)
        start_elem = jnp.clip(group_index, 0, group_count - 1) * group_width
        usable = (group_index >= 0) & (group_index < group_count)
        solved_block, first_layer = lax.cond(
            usable, backward_run_group, backward_skip_group, inbound, start_elem
        )
        updated = lax.dynamic_update_slice_in_dim(gathered, solved_block, start_elem, 1)
        return (first_layer, jnp.where(usable, updated, gathered))

    initial = (
        jnp.zeros((group_width,) + fixed_bwd.shape[2:], jnp.float32),
        jnp.zeros_like(fixed_bwd),
    )
    _, result = lax.fori_loop(0, flow_size + group_count - 1, backward_run_section, initial)
    return result


def per_device(
    right_side,
    old_state,
    block_inverse,
    flux_jacobian,
    face_lift,
    upstream,
    downstream,
    live_counts,
):
    layer_count, elem_count, unknowns = right_side.shape
    grid_shape = (layer_count, elem_count, 5, unknowns // 5)
    source = right_side.reshape(grid_shape)
    slot_index = jnp.arange(elem_count, dtype=jnp.int32)
    live = (slot_index[None, :] < live_counts).astype(jnp.float32)
    up_local = upstream % elem_count
    down_local = downstream % elem_count
    group_count = elem_count // GRP
    state_old = old_state.reshape(grid_shape) * live[:, :, None, None]
    padded_old = extended(state_old, (("cross", 1),), 1)
    next_first = passed_along(state_old[0], "flow", -1)
    following = jnp.concatenate([state_old[1:], next_first[None]], 0)
    down_old = jnp.take_along_axis(following, down_local[:, :, None, None], axis=1)
    fixed_fwd = (
        source
        - couple(down_old, face_lift[1], flux_jacobian[:, :, 1])
        - couple(padded_old[:, :-2], face_lift[2], flux_jacobian[:, :, 2])
        - couple(padded_old[:, 2:], face_lift[3], flux_jacobian[:, :, 3])
    )
    half_state, received = forward_chain(
        fixed_fwd, block_inverse, flux_jacobian[:, :, 0], face_lift[0], up_local, live, group_count
    )
    padded_half = extended(half_state, (("cross", 1),), 1)
    earlier = jnp.concatenate([received[None], half_state[:-1]], 0)
    up_new = jnp.take_along_axis(earlier, up_local[:, :, None, None], axis=1)
    fixed_bwd = (
        source
        - couple(up_new, face_lift[0], flux_jacobian[:, :, 0])
        - couple(padded_half[:, :-2], face_lift[2], flux_jacobian[:, :, 2])
        - couple(padded_half[:, 2:], face_lift[3], flux_jacobian[:, :, 3])
    )
    full_state = backward_chain(
        fixed_bwd,
        block_inverse,
        flux_jacobian[:, :, 1],
        face_lift[1],
        down_local,
        live,
        group_count,
    )
    return (half_state.reshape(right_side.shape), full_state.reshape(right_side.shape))


def solution(mesh):
    in_specs = (
        P("flow", "cross", None),
        P("flow", "cross", None),
        P("flow", "cross", None, None),
        P("flow", "cross", None, None),
        P(),
        P("flow", "cross"),
        P("flow", "cross"),
        P("flow", "cross"),
    )
    out_specs = (P("flow", "cross", None), P("flow", "cross", None))
    return jax.shard_map(
        per_device, mesh=mesh, in_specs=in_specs, out_specs=out_specs, check_vma=False
    )
```

profile of v0, /device:TPU:16, one launch (start us, length us, event | category | flops | bytes accessed | tf_op | source)
XLA Modules:
  0.0 670.0 jit_solution(8992981389225292867)
XLA Ops:
  21.5 308.3 %while.36 = (s32[]{:T(128)}, f32[4,5,64]{2,1,0:T(8,128)}, f32[1,64,5,64]{3,2,1,0:T(8,128)S(1)}, f32[64,5,64]{2,1,0:T(8,128)S(1)}, s32[]{:T(128)}, /*index=5*/bf1...) while((s32[]{:T(128)}, f32[4,5,64]{2,1,0:T(8,128)}, ...), condition=%wide.region_3.5_spmd.clone, body=%wide.region_0.4_spmd.clone.sunk | while | flops 1886624 | bytes 1201929 | solution.py:97
  106.7 6.3 collective-permute-start
  118.4 6.3 collective-permute-start
  130.0 6.3 collective-permute-start
  141.7 6.5 collective-permute-start
  153.5 6.3 collective-permute-start
  165.2 6.3 collective-permute-start
  176.8 6.3 collective-permute-start
  188.5 6.3 collective-permute-start
  197.1 9.4 %collective-permute-start = (f32[4,5,64]{2,1,0:T(8,128)}, f32[4,5,64]{2,1,0:T(8,128)S(1)}, u32[]{:S(2)}, u32[]{:S(2)}) collective-permute-start(f32[4,5,64]{2,1,0:T(8,128)} %get-tuple-element.760), channel_id=1, source_target_pairs={{0,8},{8,16},{16,24},{24,32},{32,40},{40,48},{48,56},{56,64},{64,7... | collective-permute-start | bytes 15368 | tf_op jit(solution)/shard_map/while/body/eval_jaxpr/ppermute | solution.py:15
  208.8 6.3 collective-permute-start
  217.3 9.4 %collective-permute-start = (f32[4,5,64]{2,1,0:T(8,128)}, f32[4,5,64]{2,1,0:T(8,128)S(1)}, u32[]{:S(2)}, u32[]{:S(2)}) collective-permute-start(f32[4,5,64]{2,1,0:T(8,128)} %get-tuple-element.760), channel_id=1, source_target_pairs={{0,8},{8,16},{16,24},{24,32},{32,40},{40,48},{48,56},{56,64},{64,7... | collective-permute-start | bytes 15368 | tf_op jit(solution)/shard_map/while/body/eval_jaxpr/ppermute | solution.py:15
  229.0 6.3 collective-permute-start
  237.6 9.4 %collective-permute-start = (f32[4,5,64]{2,1,0:T(8,128)}, f32[4,5,64]{2,1,0:T(8,128)S(1)}, u32[]{:S(2)}, u32[]{:S(2)}) collective-permute-start(f32[4,5,64]{2,1,0:T(8,128)} %get-tuple-element.760), channel_id=1, source_target_pairs={{0,8},{8,16},{16,24},{24,32},{32,40},{40,48},{48,56},{56,64},{64,7... | collective-permute-start | bytes 15368 | tf_op jit(solution)/shard_map/while/body/eval_jaxpr/ppermute | solution.py:15
  249.3 6.3 collective-permute-start
  257.8 9.4 %collective-permute-start = (f32[4,5,64]{2,1,0:T(8,128)}, f32[4,5,64]{2,1,0:T(8,128)S(1)}, u32[]{:S(2)}, u32[]{:S(2)}) collective-permute-start(f32[4,5,64]{2,1,0:T(8,128)} %get-tuple-element.760), channel_id=1, source_target_pairs={{0,8},{8,16},{16,24},{24,32},{32,40},{40,48},{48,56},{56,64},{64,7... | collective-permute-start | bytes 15368 | tf_op jit(solution)/shard_map/while/body/eval_jaxpr/ppermute | solution.py:15
  269.5 6.3 collective-permute-start
  278.1 6.3 collective-permute-start
  286.7 6.3 collective-permute-start
  295.3 6.3 collective-permute-start
  303.9 6.3 collective-permute-start
  312.5 6.5 collective-permute-start
  321.2 6.3 collective-permute-start
  340.5 328.6 %while.37 = (s32[]{:T(128)}, f32[4,5,64]{2,1,0:T(8,128)}, f32[1,64,5,64]{3,2,1,0:T(8,128)S(1)}, s32[]{:T(128)}, bf16[1,64,320,320]{3,2,1,0:T(8,128)(2,1)}, /*ind...) while((s32[]{:T(128)}, f32[4,5,64]{2,1,0:T(8,128)}, ...), condition=%wide.region_7.9_spmd.clone, body=%wide.region_4.8_spmd.clone.sunk | while | flops 1885344 | bytes 1152764 | solution.py:149
  342.5 6.3 collective-permute-done.1
  351.3 6.3 collective-permute-done.1
  360.2 6.3 collective-permute-done.1
  369.0 6.3 collective-permute-done.1
  463.4 6.1 collective-permute-done.1
  472.1 18.8 %collective-permute-done.1 = f32[4,5,64]{2,1,0:T(8,128)S(1)} collective-permute-done((f32[4,5,64]{2,1,0:T(8,128)}, f32[4,5,64]{2,1,0:T(8,128)S(1)}, u32[]{:S(2)}, u32[]{:S(2)}) %collective-permute-start.1) | collective-permute-done | bytes 5152 | tf_op jit(solution)/shard_map/while/body/eval_jaxpr/ppermute | solution.py:15
  566.4 6.1 collective-permute-done.1
  601.2 6.0 collective-permute-done.1
  (852 shorter events, 587.2 us)
Async XLA Ops:
  2.6 14.4 %collective-permute-start.2 = (f32[64,5,64]{2,0,1:T(8,128)S(1)}, f32[64,5,64]{2,0,1:T(8,128)S(1)}, u32[]{:S(2)}, u32[]{:S(2)}) collective-permute-start(f32[64,5,64]{2,0,1:T(8,128)S(1)} %broadcast_multiply_fusion.1), channel_id=1, source_target_pairs={{8,0},{16,8},{24,16},{32,24},{40,32},{48,40},{56,48},{64,56},{72,6... | collective-permute-start | bytes 245768 | tf_op jit(solution)/shard_map/ppermute | solution.py:15
  4.1 10.8 %collective-permute-start.3 = (f32[1,1,5,64]{3,1,2,0:T(1,128)S(1)}, f32[1,1,5,64]{3,1,2,0:T(1,128)S(1)}, u32[]{:S(2)}, u32[]{:S(2)}) collective-permute-start(f32[1,1,5,64]{3,1,2,0:T(1,128)S(1)} %get-tuple-element.591), channel_id=1, source_target_pairs={{0,1},{1,2},{2,3},{3,4},{4,5},{5,6},{6,7},{8,9},{9,10},{10,11},{11... | collective-permute-start | bytes 3848 | tf_op jit(solution)/shard_map/ppermute | solution.py:26
  6.0 9.9 %collective-permute-start.4 = (f32[1,1,5,64]{3,1,2,0:T(1,128)S(1)}, f32[1,1,5,64]{3,1,2,0:T(1,128)S(1)}, u32[]{:S(2)}, u32[]{:S(2)}) collective-permute-start(f32[1,1,5,64]{3,1,2,0:T(1,128)S(1)} %get-tuple-element.590), channel_id=1, source_target_pairs={{1,0},{2,1},{3,2},{4,3},{5,4},{6,5},{7,6},{9,8},{10,9},{11,10},{12... | collective-permute-start | bytes 3848 | tf_op jit(solution)/shard_map/ppermute | solution.py:28
  106.7 8.0 %collective-permute-start = (f32[4,5,64]{2,1,0:T(8,128)}, f32[4,5,64]{2,1,0:T(8,128)S(1)}, u32[]{:S(2)}, u32[]{:S(2)}) collective-permute-start(f32[4,5,64]{2,1,0:T(8,128)} %get-tuple-element.760), channel_id=1, source_target_pairs={{0,8},{8,16},{16,24},{24,32},{32,40},{40,48},{48,56},{56,64},{64,7... | collective-permute-start | bytes 15368 | tf_op jit(solution)/shard_map/while/body/eval_jaxpr/ppermute | solution.py:15
  118.4 8.0 %collective-permute-start = (f32[4,5,64]{2,1,0:T(8,128)}, f32[4,5,64]{2,1,0:T(8,128)S(1)}, u32[]{:S(2)}, u32[]{:S(2)}) collective-permute-start(f32[4,5,64]{2,1,0:T(8,128)} %get-tuple-element.760), channel_id=1, source_target_pairs={{0,8},{8,16},{16,24},{24,32},{32,40},{40,48},{48,56},{56,64},{64,7... | collective-permute-start | bytes 15368 | tf_op jit(solution)/shard_map/while/body/eval_jaxpr/ppermute | solution.py:15
  141.7 8.1 %collective-permute-start = (f32[4,5,64]{2,1,0:T(8,128)}, f32[4,5,64]{2,1,0:T(8,128)S(1)}, u32[]{:S(2)}, u32[]{:S(2)}) collective-permute-start(f32[4,5,64]{2,1,0:T(8,128)} %get-tuple-element.760), channel_id=1, source_target_pairs={{0,8},{8,16},{16,24},{24,32},{32,40},{40,48},{48,56},{56,64},{64,7... | collective-permute-start | bytes 15368 | tf_op jit(solution)/shard_map/while/body/eval_jaxpr/ppermute | solution.py:15
  165.2 8.0 %collective-permute-start = (f32[4,5,64]{2,1,0:T(8,128)}, f32[4,5,64]{2,1,0:T(8,128)S(1)}, u32[]{:S(2)}, u32[]{:S(2)}) collective-permute-start(f32[4,5,64]{2,1,0:T(8,128)} %get-tuple-element.760), channel_id=1, source_target_pairs={{0,8},{8,16},{16,24},{24,32},{32,40},{40,48},{48,56},{56,64},{64,7... | collective-permute-start | bytes 15368 | tf_op jit(solution)/shard_map/while/body/eval_jaxpr/ppermute | solution.py:15
  176.8 8.0 %collective-permute-start = (f32[4,5,64]{2,1,0:T(8,128)}, f32[4,5,64]{2,1,0:T(8,128)S(1)}, u32[]{:S(2)}, u32[]{:S(2)}) collective-permute-start(f32[4,5,64]{2,1,0:T(8,128)} %get-tuple-element.760), channel_id=1, source_target_pairs={{0,8},{8,16},{16,24},{24,32},{32,40},{40,48},{48,56},{56,64},{64,7... | collective-permute-start | bytes 15368 | tf_op jit(solution)/shard_map/while/body/eval_jaxpr/ppermute | solution.py:15
  197.1 11.0 %collective-permute-start = (f32[4,5,64]{2,1,0:T(8,128)}, f32[4,5,64]{2,1,0:T(8,128)S(1)}, u32[]{:S(2)}, u32[]{:S(2)}) collective-permute-start(f32[4,5,64]{2,1,0:T(8,128)} %get-tuple-element.760), channel_id=1, source_target_pairs={{0,8},{8,16},{16,24},{24,32},{32,40},{40,48},{48,56},{56,64},{64,7... | collective-permute-start | bytes 15368 | tf_op jit(solution)/shard_map/while/body/eval_jaxpr/ppermute | solution.py:15
  208.8 8.0 %collective-permute-start = (f32[4,5,64]{2,1,0:T(8,128)}, f32[4,5,64]{2,1,0:T(8,128)S(1)}, u32[]{:S(2)}, u32[]{:S(2)}) collective-permute-start(f32[4,5,64]{2,1,0:T(8,128)} %get-tuple-element.760), channel_id=1, source_target_pairs={{0,8},{8,16},{16,24},{24,32},{32,40},{40,48},{48,56},{56,64},{64,7... | collective-permute-start | bytes 15368 | tf_op jit(solution)/shard_map/while/body/eval_jaxpr/ppermute | solution.py:15
  217.3 11.0 %collective-permute-start = (f32[4,5,64]{2,1,0:T(8,128)}, f32[4,5,64]{2,1,0:T(8,128)S(1)}, u32[]{:S(2)}, u32[]{:S(2)}) collective-permute-start(f32[4,5,64]{2,1,0:T(8,128)} %get-tuple-element.760), channel_id=1, source_target_pairs={{0,8},{8,16},{16,24},{24,32},{32,40},{40,48},{48,56},{56,64},{64,7... | collective-permute-start | bytes 15368 | tf_op jit(solution)/shard_map/while/body/eval_jaxpr/ppermute | solution.py:15
  229.0 8.0 %collective-permute-start = (f32[4,5,64]{2,1,0:T(8,128)}, f32[4,5,64]{2,1,0:T(8,128)S(1)}, u32[]{:S(2)}, u32[]{:S(2)}) collective-permute-start(f32[4,5,64]{2,1,0:T(8,128)} %get-tuple-element.760), channel_id=1, source_target_pairs={{0,8},{8,16},{16,24},{24,32},{32,40},{40,48},{48,56},{56,64},{64,7... | collective-permute-start | bytes 15368 | tf_op jit(solution)/shard_map/while/body/eval_jaxpr/ppermute | solution.py:15
  237.6 11.0 %collective-permute-start = (f32[4,5,64]{2,1,0:T(8,128)}, f32[4,5,64]{2,1,0:T(8,128)S(1)}, u32[]{:S(2)}, u32[]{:S(2)}) collective-permute-start(f32[4,5,64]{2,1,0:T(8,128)} %get-tuple-element.760), channel_id=1, source_target_pairs={{0,8},{8,16},{16,24},{24,32},{32,40},{40,48},{48,56},{56,64},{64,7... | collective-permute-start | bytes 15368 | tf_op jit(solution)/shard_map/while/body/eval_jaxpr/ppermute | solution.py:15
  249.3 8.0 %collective-permute-start = (f32[4,5,64]{2,1,0:T(8,128)}, f32[4,5,64]{2,1,0:T(8,128)S(1)}, u32[]{:S(2)}, u32[]{:S(2)}) collective-permute-start(f32[4,5,64]{2,1,0:T(8,128)} %get-tuple-element.760), channel_id=1, source_target_pairs={{0,8},{8,16},{16,24},{24,32},{32,40},{40,48},{48,56},{56,64},{64,7... | collective-permute-start | bytes 15368 | tf_op jit(solution)/shard_map/while/body/eval_jaxpr/ppermute | solution.py:15
  257.8 11.0 %collective-permute-start = (f32[4,5,64]{2,1,0:T(8,128)}, f32[4,5,64]{2,1,0:T(8,128)S(1)}, u32[]{:S(2)}, u32[]{:S(2)}) collective-permute-start(f32[4,5,64]{2,1,0:T(8,128)} %get-tuple-element.760), channel_id=1, source_target_pairs={{0,8},{8,16},{16,24},{24,32},{32,40},{40,48},{48,56},{56,64},{64,7... | collective-permute-start | bytes 15368 | tf_op jit(solution)/shard_map/while/body/eval_jaxpr/ppermute | solution.py:15
  269.5 8.0 %collective-permute-start = (f32[4,5,64]{2,1,0:T(8,128)}, f32[4,5,64]{2,1,0:T(8,128)S(1)}, u32[]{:S(2)}, u32[]{:S(2)}) collective-permute-start(f32[4,5,64]{2,1,0:T(8,128)} %get-tuple-element.760), channel_id=1, source_target_pairs={{0,8},{8,16},{16,24},{24,32},{32,40},{40,48},{48,56},{56,64},{64,7... | collective-permute-start | bytes 15368 | tf_op jit(solution)/shard_map/while/body/eval_jaxpr/ppermute | solution.py:15
  278.1 8.0 %collective-permute-start = (f32[4,5,64]{2,1,0:T(8,128)}, f32[4,5,64]{2,1,0:T(8,128)S(1)}, u32[]{:S(2)}, u32[]{:S(2)}) collective-permute-start(f32[4,5,64]{2,1,0:T(8,128)} %get-tuple-element.760), channel_id=1, source_target_pairs={{0,8},{8,16},{16,24},{24,32},{32,40},{40,48},{48,56},{56,64},{64,7... | collective-permute-start | bytes 15368 | tf_op jit(solution)/shard_map/while/body/eval_jaxpr/ppermute | solution.py:15
  286.7 8.0 %collective-permute-start = (f32[4,5,64]{2,1,0:T(8,128)}, f32[4,5,64]{2,1,0:T(8,128)S(1)}, u32[]{:S(2)}, u32[]{:S(2)}) collective-permute-start(f32[4,5,64]{2,1,0:T(8,128)} %get-tuple-element.760), channel_id=1, source_target_pairs={{0,8},{8,16},{16,24},{24,32},{32,40},{40,48},{48,56},{56,64},{64,7... | collective-permute-start | bytes 15368 | tf_op jit(solution)/shard_map/while/body/eval_jaxpr/ppermute | solution.py:15
  295.3 8.0 %collective-permute-start = (f32[4,5,64]{2,1,0:T(8,128)}, f32[4,5,64]{2,1,0:T(8,128)S(1)}, u32[]{:S(2)}, u32[]{:S(2)}) collective-permute-start(f32[4,5,64]{2,1,0:T(8,128)} %get-tuple-element.760), channel_id=1, source_target_pairs={{0,8},{8,16},{16,24},{24,32},{32,40},{40,48},{48,56},{56,64},{64,7... | collective-permute-start | bytes 15368 | tf_op jit(solution)/shard_map/while/body/eval_jaxpr/ppermute | solution.py:15
  303.9 8.0 %collective-permute-start = (f32[4,5,64]{2,1,0:T(8,128)}, f32[4,5,64]{2,1,0:T(8,128)S(1)}, u32[]{:S(2)}, u32[]{:S(2)}) collective-permute-start(f32[4,5,64]{2,1,0:T(8,128)} %get-tuple-element.760), channel_id=1, source_target_pairs={{0,8},{8,16},{16,24},{24,32},{32,40},{40,48},{48,56},{56,64},{64,7... | collective-permute-start | bytes 15368 | tf_op jit(solution)/shard_map/while/body/eval_jaxpr/ppermute | solution.py:15
  312.5 8.1 %collective-permute-start = (f32[4,5,64]{2,1,0:T(8,128)}, f32[4,5,64]{2,1,0:T(8,128)S(1)}, u32[]{:S(2)}, u32[]{:S(2)}) collective-permute-start(f32[4,5,64]{2,1,0:T(8,128)} %get-tuple-element.760), channel_id=1, source_target_pairs={{0,8},{8,16},{16,24},{24,32},{32,40},{40,48},{48,56},{56,64},{64,7... | collective-permute-start | bytes 15368 | tf_op jit(solution)/shard_map/while/body/eval_jaxpr/ppermute | solution.py:15
  329.9 8.2 %collective-permute-start.5 = (f32[1,1,5,64]{3,1,2,0:T(1,128)S(1)}, f32[1,1,5,64]{3,1,2,0:T(1,128)S(1)}, u32[]{:S(2)}, u32[]{:S(2)}) collective-permute-start(f32[1,1,5,64]{3,1,2,0:T(1,128)S(1)} %get-tuple-element.589), channel_id=1, source_target_pairs={{0,1},{1,2},{2,3},{3,4},{4,5},{5,6},{6,7},{8,9},{9,10},{10,11},{11... | collective-permute-start | bytes 3848 | tf_op jit(solution)/shard_map/ppermute | solution.py:26
  340.5 8.2 %collective-permute-start.1 = (f32[4,5,64]{2,1,0:T(8,128)}, f32[4,5,64]{2,1,0:T(8,128)S(1)}, u32[]{:S(2)}, u32[]{:S(2)}) collective-permute-start(f32[4,5,64]{2,1,0:T(8,128)} %get-tuple-element.810), channel_id=1, source_target_pairs={{8,0},{16,8},{24,16},{32,24},{40,32},{48,40},{56,48},{64,56},{72,6... | collective-permute-start | bytes 15368 | tf_op jit(solution)/shard_map/while/body/eval_jaxpr/ppermute | solution.py:15
  349.4 8.2 %collective-permute-start.1 = (f32[4,5,64]{2,1,0:T(8,128)}, f32[4,5,64]{2,1,0:T(8,128)S(1)}, u32[]{:S(2)}, u32[]{:S(2)}) collective-permute-start(f32[4,5,64]{2,1,0:T(8,128)} %get-tuple-element.810), channel_id=1, source_target_pairs={{8,0},{16,8},{24,16},{32,24},{40,32},{48,40},{56,48},{64,56},{72,6... | collective-permute-start | bytes 15368 | tf_op jit(solution)/shard_map/while/body/eval_jaxpr/ppermute | solution.py:15
  358.2 8.2 %collective-permute-start.1 = (f32[4,5,64]{2,1,0:T(8,128)}, f32[4,5,64]{2,1,0:T(8,128)S(1)}, u32[]{:S(2)}, u32[]{:S(2)}) collective-permute-start(f32[4,5,64]{2,1,0:T(8,128)} %get-tuple-element.810), channel_id=1, source_target_pairs={{8,0},{16,8},{24,16},{32,24},{40,32},{48,40},{56,48},{64,56},{72,6... | collective-permute-start | bytes 15368 | tf_op jit(solution)/shard_map/while/body/eval_jaxpr/ppermute | solution.py:15
  367.1 8.2 %collective-permute-start.1 = (f32[4,5,64]{2,1,0:T(8,128)}, f32[4,5,64]{2,1,0:T(8,128)S(1)}, u32[]{:S(2)}, u32[]{:S(2)}) collective-permute-start(f32[4,5,64]{2,1,0:T(8,128)} %get-tuple-element.810), channel_id=1, source_target_pairs={{8,0},{16,8},{24,16},{32,24},{40,32},{48,40},{56,48},{64,56},{72,6... | collective-permute-start | bytes 15368 | tf_op jit(solution)/shard_map/while/body/eval_jaxpr/ppermute | solution.py:15
  410.1 8.0 %collective-permute-start.1 = (f32[4,5,64]{2,1,0:T(8,128)}, f32[4,5,64]{2,1,0:T(8,128)S(1)}, u32[]{:S(2)}, u32[]{:S(2)}) collective-permute-start(f32[4,5,64]{2,1,0:T(8,128)} %get-tuple-element.810), channel_id=1, source_target_pairs={{8,0},{16,8},{24,16},{32,24},{40,32},{48,40},{56,48},{64,56},{72,6... | collective-permute-start | bytes 15368 | tf_op jit(solution)/shard_map/while/body/eval_jaxpr/ppermute | solution.py:15
  461.5 8.0 %collective-permute-start.1 = (f32[4,5,64]{2,1,0:T(8,128)}, f32[4,5,64]{2,1,0:T(8,128)S(1)}, u32[]{:S(2)}, u32[]{:S(2)}) collective-permute-start(f32[4,5,64]{2,1,0:T(8,128)} %get-tuple-element.810), channel_id=1, source_target_pairs={{8,0},{16,8},{24,16},{32,24},{40,32},{48,40},{56,48},{64,56},{72,6... | collective-permute-start | bytes 15368 | tf_op jit(solution)/shard_map/while/body/eval_jaxpr/ppermute | solution.py:15
  470.1 20.8 %collective-permute-start.1 = (f32[4,5,64]{2,1,0:T(8,128)}, f32[4,5,64]{2,1,0:T(8,128)S(1)}, u32[]{:S(2)}, u32[]{:S(2)}) collective-permute-start(f32[4,5,64]{2,1,0:T(8,128)} %get-tuple-element.810), channel_id=1, source_target_pairs={{8,0},{16,8},{24,16},{32,24},{40,32},{48,40},{56,48},{64,56},{72,6... | collective-permute-start | bytes 15368 | tf_op jit(solution)/shard_map/while/body/eval_jaxpr/ppermute | solution.py:15
  517.9 8.0 %collective-permute-start.1 = (f32[4,5,64]{2,1,0:T(8,128)}, f32[4,5,64]{2,1,0:T(8,128)S(1)}, u32[]{:S(2)}, u32[]{:S(2)}) collective-permute-start(f32[4,5,64]{2,1,0:T(8,128)} %get-tuple-element.810), channel_id=1, source_target_pairs={{8,0},{16,8},{24,16},{32,24},{40,32},{48,40},{56,48},{64,56},{72,6... | collective-permute-start | bytes 15368 | tf_op jit(solution)/shard_map/while/body/eval_jaxpr/ppermute | solution.py:15
  564.4 8.0 %collective-permute-start.1 = (f32[4,5,64]{2,1,0:T(8,128)}, f32[4,5,64]{2,1,0:T(8,128)S(1)}, u32[]{:S(2)}, u32[]{:S(2)}) collective-permute-start(f32[4,5,64]{2,1,0:T(8,128)} %get-tuple-element.810), channel_id=1, source_target_pairs={{8,0},{16,8},{24,16},{32,24},{40,32},{48,40},{56,48},{64,56},{72,6... | collective-permute-start | bytes 15368 | tf_op jit(solution)/shard_map/while/body/eval_jaxpr/ppermute | solution.py:15
  599.3 8.0 %collective-permute-start.1 = (f32[4,5,64]{2,1,0:T(8,128)}, f32[4,5,64]{2,1,0:T(8,128)S(1)}, u32[]{:S(2)}, u32[]{:S(2)}) collective-permute-start(f32[4,5,64]{2,1,0:T(8,128)} %get-tuple-element.810), channel_id=1, source_target_pairs={{8,0},{16,8},{24,16},{32,24},{40,32},{48,40},{56,48},{64,56},{72,6... | collective-permute-start | bytes 15368 | tf_op jit(solution)/shard_map/while/body/eval_jaxpr/ppermute | solution.py:15
  (36 other events, 588.3 us)
where the time goes:
time: 674 us; the launch traced here: 670 us
  starting transfers between devices  241 us (36%)
  waiting for transfers between devices  229 us (34%)
  local copies, waits for them, and re-layouts  78.1 us (12%)
  matrix products  69.2 us (10%)
  other arithmetic  47.6 us (7%)
    ppermute x63, starting transfers between devices, passed_along(): return lax.ppermute(block, axis, route)  229 us
    ppermute x63, waiting for transfers between devices, passed_along(): return lax.ppermute(block, axis, route)  229 us
    dot_general x32, matrix products, solve_blocks(): jnp.einsum('...ij,...j->...i', inverse, flat, preferred_element_type=jnp....  50.5 us
    convert_element_type x63, other arithmetic, per_device(): live = (slot_index[None, :] < live_counts).astype(jnp.float32)  40.4 us
    reshape x32, local copies, waits for them, and re-layouts, solve_blocks(): return (solved * live[..., None]).reshape(residual.shape)  22.3 us
    another operation x70, local copies, waits for them, and re-layouts  20.1 us
  transfers between devices with their start and end apart: 67, of which 62 were waited for; matrix products, arithmetic and copies ran while one was open for 8% of the time, Pallas kernels for 0%

commit v1 on v0

v1 whole, which is shorter than its diff:
```python
import functools

import jax
import jax.numpy as jnp
from jax import lax
from jax.experimental import pallas as pl
from jax.experimental.pallas import tpu as pltpu
from jax.sharding import PartitionSpec as P

GROUPS = 4
NVAR = 5
NB = 64
WIDE = 384
STEP_VMEM = 4 << 20
PREP_VMEM = 12 << 20

VMEM_SPEC = pl.BlockSpec(memory_space=pltpu.VMEM)
SMEM_SPEC = pl.BlockSpec(memory_space=pltpu.SMEM)


def dot(a, b):
    return jnp.dot(a, b, preferred_element_type=jnp.float32)


def split(x):
    high = x.astype(jnp.bfloat16)
    low = (x - high.astype(jnp.float32)).astype(jnp.bfloat16)
    return high, low


def couple(x, lift_high, lift_low, mix):
    m = x.shape[0]
    stacked = jnp.concatenate([x[:, :128], x[:, 128:256], x[:, 256:]], axis=0)
    high, low = split(stacked)
    spread = dot(jnp.concatenate([high, low], axis=1), lift_high) + dot(high, lift_low)
    parts = [spread[v // 2 * m : v // 2 * m + m, v % 2 * 128 : v % 2 * 128 + 128] for v in range(NVAR)]
    chunks = []
    for k in range(3):
        at = slice(128 * k, 128 * k + 128)
        total = mix[0][:, at] * parts[0]
        for v in range(1, NVAR):
            total = total + mix[v][:, at] * parts[v]
        chunks.append(total)
    return jnp.concatenate(chunks, axis=1)


def padded(x):
    return jnp.concatenate([x, jnp.zeros((x.shape[0], WIDE - x.shape[1]), x.dtype)], axis=1)


def setup_kernel(
    down_ref, rhs_ref, old_ref, next_ref, left_ref, right_ref, flux_ref, lift_ref,
    fixed_ref, source_ref, mix_ref, high_ref, low_ref, shift_ref, gather_ref,
):
    elems = rhs_ref.shape[0]
    lane = lax.broadcasted_iota(jnp.int32, (elems, 128), 1)
    for d in range(4):
        lift_t = lift_ref[d].T
        both = jnp.concatenate([lift_t, lift_t], axis=1)
        none = jnp.zeros_like(both)
        weight = jnp.concatenate(
            [jnp.concatenate([both, none], axis=1), jnp.concatenate([none, both], axis=1)], axis=0
        )
        high, low = split(weight)
        high_ref[d] = jnp.concatenate([high, high], axis=0)
        low_ref[d] = low
        flux = flux_ref[d]
        for v in range(NVAR):
            for k in range(3):
                u = 2 * k
                first = jnp.broadcast_to(flux[:, 5 * u + v : 5 * u + v + 1], (elems, 128))
                if u + 1 < NVAR:
                    at = 5 * (u + 1) + v
                    second = jnp.broadcast_to(flux[:, at : at + 1], (elems, 128))
                else:
                    second = jnp.zeros((elems, 128), jnp.float32)
                mix_ref[d, v, :, 128 * k : 128 * k + 128] = jnp.where(lane < NB, first, second)
    shift_ref[0:8, :] = jnp.zeros((8, WIDE), jnp.float32)
    shift_ref[elems + 8 : elems + 16, :] = jnp.zeros((8, WIDE), jnp.float32)
    shift_ref[8 : elems + 8, :] = padded(old_ref[...])
    shift_ref[7:8, :] = padded(left_ref[...])
    shift_ref[elems + 8 : elems + 9, :] = padded(right_ref[...])
    gather_ref[...] = jnp.zeros_like(gather_ref)
    for e in range(elems):
        gather_ref[e : e + 1, 0:320] = next_ref[pl.ds(down_ref[0, e], 1), :]
    source = padded(rhs_ref[...])
    source_ref[...] = source

    def face(x, d):
        return couple(x, high_ref[d], low_ref[d], [mix_ref[d, v] for v in range(NVAR)])

    fixed = source - face(gather_ref[...], 1)
    fixed = fixed - face(shift_ref[7 : elems + 7, :], 2)
    fixed_ref[...] = fixed - face(shift_ref[9 : elems + 9, :], 3)


def collect(width, place_ref, parts, out_ref, offset):
    for s, part_ref in enumerate(parts):
        position = s - place_ref[0]

        @pl.when((position >= 0) & (position < GROUPS))
        def _():
            rows = pl.ds(pl.multiple_of(position * width, width) + offset, width)
            out_ref[rows, :] = part_ref[...][:, : out_ref.shape[1]]


def collect_kernel(steps, width, place_ref, *refs):
    collect(width, place_ref, refs[:steps], refs[steps], 0)


def turn_kernel(
    steps, width, place_ref, source_ref, left_ref, right_ref, mix_ref, high_ref, low_ref, *refs
):
    halves, uppers, (fixed_ref, shift_ref, upper_ref) = refs[:steps], refs[steps:2 * steps], refs[2 * steps:]
    elems = source_ref.shape[0]
    shift_ref[0:8, :] = jnp.zeros((8, WIDE), jnp.float32)
    shift_ref[elems + 8 : elems + 16, :] = jnp.zeros((8, WIDE), jnp.float32)
    collect(width, place_ref, halves, shift_ref, 8)
    collect(width, place_ref, uppers, upper_ref, 0)
    shift_ref[7:8, :] = padded(left_ref[...])
    shift_ref[elems + 8 : elems + 9, :] = padded(right_ref[...])

    def face(x, d):
        return couple(x, high_ref[d], low_ref[d], [mix_ref[d, v] for v in range(NVAR)])

    fixed = source_ref[...] - upper_ref[...]
    fixed = fixed - face(shift_ref[7 : elems + 7, :], 2)
    fixed_ref[...] = fixed - face(shift_ref[9 : elems + 9, :], 3)


def step_kernel(
    first_step, sign, face, width, groups,
    place_ref, order_ref, count_ref, message_ref, inverse_ref, fixed_ref, mix_ref, high_ref, low_ref,
    out_ref, state_ref, upper_ref,
):
    position = first_step - sign * place_ref[0]

    @pl.when((position >= 0) & (position < groups))
    def _():
        base = pl.multiple_of(position * width, width)
        rows = pl.ds(base, width)
        mix = [mix_ref[face, v, rows, :] for v in range(NVAR)]
        inflow = couple(message_ref[...], high_ref[face], low_ref[face], mix)
        upper_ref[...] = inflow
        resid = (fixed_ref[rows, :] - inflow)[:, :320].astype(jnp.bfloat16)
        row = lax.broadcasted_iota(jnp.int32, (width, 320), 0)
        solved = jnp.zeros((width, 320), jnp.float32)
        for e in range(width):
            product = lax.dot_general(
                resid, inverse_ref[base + e], (((1,), (1,)), ((), ())),
                preferred_element_type=jnp.float32,
            )
            solved = jnp.where(row == e, product, solved)
        solved = jnp.where(row + base < count_ref[0, 0], solved, 0.0)
        wide = padded(solved)
        state_ref[...] = wide
        for e in range(width):
            out_ref[pl.ds(order_ref[0, base + e] - base, 1), :] = wide[e : e + 1, :]


def step_call(first_step, sign, face, width, groups):
    body = functools.partial(step_kernel, first_step, sign, face, width, groups)
    return pl.pallas_call(
        body,
        out_shape=(jax.ShapeDtypeStruct((width, WIDE), jnp.float32),) * 3,
        in_specs=[SMEM_SPEC] * 3 + [VMEM_SPEC] * 6,
        out_specs=(VMEM_SPEC,) * 3,
        compiler_params=pltpu.CompilerParams(vmem_limit_bytes=STEP_VMEM),
        name="sweep_step",
    )


def edge_rows(cells):
    count = lax.axis_size("cross")
    right = [(i, i + 1) for i in range(count - 1)]
    left = [(i + 1, i) for i in range(count - 1)]
    return lax.ppermute(cells[-1:], "cross", right), lax.ppermute(cells[:1], "cross", left)


def sweep(order, count, place, fixed, inverse, mix, high, low, face, sign, layers):
    elems = fixed.shape[0]
    width = elems // GROUPS
    message = jnp.zeros((width, WIDE), jnp.float32)
    states, uppers = [], []
    for s in range(layers + GROUPS - 1):
        first = s if sign > 0 else s - (layers - 1)
        call = step_call(first, sign, face, width, GROUPS)
        out, state, upper = call(place, order, count, message, inverse, fixed, mix, high, low)
        states.append(state)
        uppers.append(upper)
        turn = [l for l in range(layers - 1) if 0 <= s - l < GROUPS]
        if sign > 0:
            route = [(l, l + 1) for l in turn]
        else:
            route = [(layers - 1 - l, layers - 2 - l) for l in turn]
        if route:
            message = lax.ppermute(out, "flow", route)
    return states, uppers


def collected(place, states, elems):
    steps = len(states)
    body = functools.partial(collect_kernel, steps, elems // GROUPS)
    return pl.pallas_call(
        body,
        out_shape=jax.ShapeDtypeStruct((elems, 320), jnp.float32),
        in_specs=[SMEM_SPEC] + [VMEM_SPEC] * steps,
        out_specs=VMEM_SPEC,
        compiler_params=pltpu.CompilerParams(vmem_limit_bytes=STEP_VMEM),
        name="sweep_collect",
    )(place, *states)


def per_device(
    right_side, old_state, block_inverse, flux_jacobian, face_lift, upstream, downstream, live_counts
):
    layers = lax.axis_size("flow")
    rhs = right_side[0]
    elems = rhs.shape[0]
    inverse = block_inverse[0]
    up = upstream % elems
    down = downstream % elems
    place = lax.axis_index("flow").reshape(1).astype(jnp.int32)
    slot = jnp.arange(elems, dtype=jnp.int32)
    old = jnp.where((slot < live_counts[0, 0])[:, None], old_state[0], 0.0)
    following = lax.ppermute(old, "flow", [(l + 1, l) for l in range(layers - 1)])
    left, right = edge_rows(old)
    flux = jnp.transpose(flux_jacobian[0], (1, 0, 2))
    f32 = jnp.float32
    shift = pltpu.VMEM((elems + 16, WIDE), f32)
    fixed, source, mix, high, low = pl.pallas_call(
        setup_kernel,
        out_shape=(
            jax.ShapeDtypeStruct((elems, WIDE), f32),
            jax.ShapeDtypeStruct((elems, WIDE), f32),
            jax.ShapeDtypeStruct((4, NVAR, elems, WIDE), f32),
            jax.ShapeDtypeStruct((4, 256, 256), jnp.bfloat16),
            jax.ShapeDtypeStruct((4, 128, 256), jnp.bfloat16),
        ),
        in_specs=[SMEM_SPEC] + [VMEM_SPEC] * 7,
        out_specs=(VMEM_SPEC,) * 5,
        scratch_shapes=[shift, pltpu.VMEM((elems, WIDE), f32)],
        compiler_params=pltpu.CompilerParams(vmem_limit_bytes=PREP_VMEM),
        name="sweep_setup",
    )(down, rhs, old, following, left, right, flux, face_lift)
    halves, uppers = sweep(
        down, live_counts, place, fixed, inverse, mix, high, low, 0, 1, layers
    )
    half = collected(place, halves, elems)
    left, right = edge_rows(half)
    steps = len(halves)
    fixed_bwd = pl.pallas_call(
        functools.partial(turn_kernel, steps, elems // GROUPS),
        out_shape=jax.ShapeDtypeStruct((elems, WIDE), f32),
        in_specs=[SMEM_SPEC] + [VMEM_SPEC] * (6 + 2 * steps),
        out_specs=VMEM_SPEC,
        scratch_shapes=[shift, pltpu.VMEM((elems, WIDE), f32)],
        compiler_params=pltpu.CompilerParams(vmem_limit_bytes=PREP_VMEM),
        name="sweep_turn",
    )(place, source, left, right, mix, high, low, *halves, *uppers)
    fulls, _ = sweep(
        up, live_counts, place, fixed_bwd, inverse, mix, high, low, 1, -1, layers
    )
    full = collected(layers - 1 - place, fulls, elems)
    return half[None], full[None]


def solution(mesh):
    in_specs = (
        P("flow", "cross", None),
        P("flow", "cross", None),
        P("flow", "cross", None, None),
        P("flow", "cross", None, None),
        P(),
        P("flow", "cross"),
        P("flow", "cross"),
        P("flow", "cross"),
    )
    out_specs = (P("flow", "cross", None), P("flow", "cross", None))
    return jax.shard_map(
        per_device, mesh=mesh, in_specs=in_specs, out_specs=out_specs, check_vma=False
    )
```

time: 674 us -> 335 us (0.50)
  waiting for transfers between devices: 229 us -> 91.5 us
  matrix products: 69.2 us -> 0 us
  local copies, waits for them, and re-layouts: 78.1 us -> 8.91 us
  starting transfers between devices: 241 us -> 181 us
  Pallas kernels: 0 us -> 48 us
  other arithmetic: 47.6 us -> 1.65 us
    ppermute x67 -> x41, waiting for transfers between devices: 229 us -> 91.5 us  [the longest x36 90.2 us: sweep(): message = lax.ppermute(out, 'flow', route)]
    dot_general x108 -> x0, matrix products: 69.2 us -> none  [the longest x32 50.5 us: solve_blocks(): jnp.einsum('...ij,...j->...i', inverse, flat, preferred_element_type=jnp....]
    ppermute x67 -> x41, starting transfers between devices: 241 us -> 181 us  [the longest x36 160 us: sweep(): message = lax.ppermute(out, 'flow', route)]
    pallas_call x0 -> x42, Pallas kernels: none -> 48 us  [the longest x38 44.1 us: sweep(): call(place, order, count, message, inverse, fixed, mix, high, low)]
    convert_element_type x63 -> x0, other arithmetic: 40.4 us -> none  [per_device(): live = (slot_index[None, :] < live_counts).astype(jnp.float32)]
    reshape x67 -> x0, local copies, waits for them, and re-layouts: 25.3 us -> none  [the longest x32 22.3 us: solve_blocks(): return (solved * live[..., None]).reshape(residual.shape)]
    another operation x71 -> x1, local copies, waits for them, and re-layouts: 20.2 us -> 0.01 us
    gather x34 -> x0, local copies, waits for them, and re-layouts: 18.8 us -> none  [the longest x16 8.78 us: backward_run_group(): nearest = later[index_part[layer_pos]]]
  transfers between devices with their start and end apart: 67 -> 41, of which waited for: 62 -> 9; matrix products, arithmetic and copies ran while one was open for 8% -> 0% of each run, Pallas kernels for 0% -> 0%
where the time goes in v1:
time: 335 us; the launch traced here: 333 us
  starting transfers between devices  181 us (54%)
  waiting for transfers between devices  91.5 us (27%)
  Pallas kernels  48 us (14%)
  local copies, waits for them, and re-layouts  8.91 us (3%)
    ppermute x36, starting transfers between devices, sweep(): message = lax.ppermute(out, 'flow', route)  160 us
    ppermute x36, waiting for transfers between devices, sweep(): message = lax.ppermute(out, 'flow', route)  90.2 us
    pallas_call x38, Pallas kernels, sweep(): call(place, order, count, message, inverse, fixed, mix, high, low)  44.1 us
    ppermute x1, starting transfers between devices, per_device(): lax.ppermute(old, 'flow', [(l + 1, l) for l in range(layers - 1)])  10.1 us
    unnamed x11, local copies, waits for them, and re-layouts  8.18 us
    ppermute x2, starting transfers between devices, edge_rows(): lax.ppermute(cells[:1], 'cross', left)  7.08 us
  transfers between devices with their start and end apart: 41, of which 9 were waited for; matrix products, arithmetic and copies ran while one was open for 0% of the time, Pallas kernels for 0%

profile of v1, /device:TPU:16, one launch (start us, length us, event | category | flops | bytes accessed | tf_op | source)
XLA Modules:
  0.0 333.5 jit_solution(11198805172464544465)
XLA Ops:
  2.3 10.1 %collective-permute-start = (f32[64,320]{1,0:T(8,128)S(1)}, f32[64,320]{1,0:T(8,128)S(1)}, u32[]{:S(2)}, u32[]{:S(2)}) collective-permute-start(f32[64,320]{1,0:T(8,128)S(1)} %bitcast_select_fusion.old_ref), channel_id=1, source_target_pairs={{8,0},{16,8},{24,16},{32,24},{40,32},{48,40},{56,48},{64,56},{72,6... | collective-permute-start | bytes 245768 | tf_op jit(solution)/shard_map/ppermute | solution.py:226
  12.4 2.0 collective-permute-start.1
  14.4 3.5 %collective-permute-start.2 = (f32[1,320]{1,0:T(1,128)S(1)}, f32[1,320]{1,0:T(1,128)S(1)}, u32[]{:S(2)}, u32[]{:S(2)}) collective-permute-start(f32[1,320]{1,0:T(1,128)S(1)} %get-tuple-element.200), channel_id=1, source_target_pairs={{1,0},{2,1},{3,2},{4,3},{5,4},{6,5},{7,6},{9,8},{10,9},{11,10},{12... | collective-permute-start | bytes 3848 | tf_op jit(solution)/shard_map/ppermute | solution.py:177
  21.4 1.8 sweep_setup.1
  23.2 5.5 %copy-done = bf16[1,64,320,320]{3,2,1,0:T(8,128)(2,1)S(1)} copy-done((bf16[1,64,320,320]{3,2,1,0:T(8,128)(2,1)S(1)}, bf16[1,64,320,320]{3,2,1,0:T(8,128)(2,1)}, u32[]{:S(2)}) %copy-start) | copy-done | bytes 13107224
  28.7 1.9 sweep_step.38
  30.6 3.3 collective-permute-start.3
  33.9 1.6 collective-permute-done.3.message_ref
  35.5 1.9 sweep_step.39
  37.4 4.4 %collective-permute-start.4 = (f32[16,384]{1,0:T(8,128)S(1)}, f32[16,384]{1,0:T(8,128)S(1)}, u32[]{:S(2)}, u32[]{:S(2)}) collective-permute-start(f32[16,384]{1,0:T(8,128)S(1)} %get-tuple-element.107), channel_id=1, source_target_pairs={{0,8},{8,16},{1,9},{9,17},{2,10},{10,18},{3,11},{11,19},{4,12},{12... | collective-permute-start | bytes 73736 | tf_op jit(solution)/shard_map/ppermute | solution.py:197
  41.8 1.5 collective-permute-done.4.message_ref
  43.3 1.9 sweep_step.40
  45.2 4.2 %collective-permute-start.5 = (f32[16,384]{1,0:T(8,128)S(1)}, f32[16,384]{1,0:T(8,128)S(1)}, u32[]{:S(2)}, u32[]{:S(2)}) collective-permute-start(f32[16,384]{1,0:T(8,128)S(1)} %get-tuple-element.109), channel_id=1, source_target_pairs={{0,8},{8,16},{16,24},{1,9},{9,17},{17,25},{2,10},{10,18},{18,26},{... | collective-permute-start | bytes 73736 | tf_op jit(solution)/shard_map/ppermute | solution.py:197
  49.4 1.5 collective-permute-done.5.message_ref
  50.9 1.9 sweep_step.41
  52.8 4.2 %collective-permute-start.6 = (f32[16,384]{1,0:T(8,128)S(1)}, f32[16,384]{1,0:T(8,128)S(1)}, u32[]{:S(2)}, u32[]{:S(2)}) collective-permute-start(f32[16,384]{1,0:T(8,128)S(1)} %get-tuple-element.111), channel_id=1, source_target_pairs={{0,8},{8,16},{16,24},{24,32},{1,9},{9,17},{17,25},{25,33},{2,10},{... | collective-permute-start | bytes 73736 | tf_op jit(solution)/shard_map/ppermute | solution.py:197
  57.0 1.5 collective-permute-done.6.message_ref
  71.7 69.8 %collective-permute-start.17 = (f32[16,384]{1,0:T(8,128)S(1)}, f32[16,384]{1,0:T(8,128)S(1)}, u32[]{:S(2)}, u32[]{:S(2)}) collective-permute-start(f32[16,384]{1,0:T(8,128)S(1)} %get-tuple-element.133), channel_id=1, source_target_pairs={{88,96},{96,104},{104,112},{112,120},{89,97},{97,105},{105,113},{1... | collective-permute-start | bytes 73736 | tf_op jit(solution)/shard_map/ppermute | solution.py:197
  147.9 2.0 collective-permute-start.21
  149.9 3.5 %collective-permute-start.22 = (f32[1,320]{1,0:T(1,128)S(1)}, f32[1,320]{1,0:T(1,128)S(1)}, u32[]{:S(2)}, u32[]{:S(2)}) collective-permute-start(f32[1,320]{1,0:T(1,128)S(1)} %get-tuple-element.198), channel_id=1, source_target_pairs={{1,0},{2,1},{3,2},{4,3},{5,4},{6,5},{7,6},{9,8},{10,9},{11,10},{12... | collective-permute-start | bytes 3848 | tf_op jit(solution)/shard_map/ppermute | solution.py:177
  162.0 51.8 %collective-permute-start.26 = (f32[16,384]{1,0:T(8,128)S(1)}, f32[16,384]{1,0:T(8,128)S(1)}, u32[]{:S(2)}, u32[]{:S(2)}) collective-permute-start(f32[16,384]{1,0:T(8,128)S(1)} %get-tuple-element.168), channel_id=1, source_target_pairs={{120,112},{112,104},{104,96},{96,88},{121,113},{113,105},{105,97},... | collective-permute-start | bytes 73736 | tf_op jit(solution)/shard_map/ppermute | solution.py:197
  233.5 1.3 collective-permute-start.37
  234.8 66.5 %collective-permute-done.37.message_ref = f32[16,384]{1,0:T(8,128)S(1)} collective-permute-done((f32[16,384]{1,0:T(8,128)S(1)}, f32[16,384]{1,0:T(8,128)S(1)}, u32[]{:S(2)}, u32[]{:S(2)}) %collective-permute-start.37) | collective-permute-done | bytes 24608 | tf_op jit(solution)/shard_map/ppermute | solution.py:197
  301.4 2.5 sweep_step.72
  303.9 1.3 collective-permute-start.38
  305.2 6.3 %collective-permute-done.38.message_ref = f32[16,384]{1,0:T(8,128)S(1)} collective-permute-done((f32[16,384]{1,0:T(8,128)S(1)}, f32[16,384]{1,0:T(8,128)S(1)}, u32[]{:S(2)}, u32[]{:S(2)}) %collective-permute-start.38) | collective-permute-done | bytes 24608 | tf_op jit(solution)/shard_map/ppermute | solution.py:197
  311.5 2.5 sweep_step.73
  314.0 1.3 collective-permute-start.39
  315.3 6.5 %collective-permute-done.39.message_ref = f32[16,384]{1,0:T(8,128)S(1)} collective-permute-done((f32[16,384]{1,0:T(8,128)S(1)}, f32[16,384]{1,0:T(8,128)S(1)}, u32[]{:S(2)}, u32[]{:S(2)}) %collective-permute-start.39) | collective-permute-done | bytes 24608 | tf_op jit(solution)/shard_map/ppermute | solution.py:197
  321.9 2.5 sweep_step.74
  325.7 4.7 %collective-permute-done.40.message_ref = f32[16,384]{1,0:T(8,128)S(1)} collective-permute-done((f32[16,384]{1,0:T(8,128)S(1)}, f32[16,384]{1,0:T(8,128)S(1)}, u32[]{:S(2)}, u32[]{:S(2)}) %collective-permute-start.40) | collective-permute-done | bytes 24608 | tf_op jit(solution)/shard_map/ppermute | solution.py:197
  330.3 2.5 sweep_step.75
  (110 shorter events, 53.6 us)
Async XLA Ops:
  2.3 17.3 %collective-permute-start = (f32[64,320]{1,0:T(8,128)S(1)}, f32[64,320]{1,0:T(8,128)S(1)}, u32[]{:S(2)}, u32[]{:S(2)}) collective-permute-start(f32[64,320]{1,0:T(8,128)S(1)} %bitcast_select_fusion.old_ref), channel_id=1, source_target_pairs={{8,0},{16,8},{24,16},{32,24},{40,32},{48,40},{56,48},{64,56},{72,6... | collective-permute-start | bytes 245768 | tf_op jit(solution)/shard_map/ppermute | solution.py:226
  12.4 7.2 %collective-permute-start.1 = (f32[1,320]{1,0:T(1,128)S(1)}, f32[1,320]{1,0:T(1,128)S(1)}, u32[]{:S(2)}, u32[]{:S(2)}) collective-permute-start(f32[1,320]{1,0:T(1,128)S(1)} %get-tuple-element.201), channel_id=1, source_target_pairs={{0,1},{1,2},{2,3},{3,4},{4,5},{5,6},{6,7},{8,9},{9,10},{10,11},{11... | collective-permute-start | bytes 3848 | tf_op jit(solution)/shard_map/ppermute | solution.py:177
  14.4 5.1 %collective-permute-start.2 = (f32[1,320]{1,0:T(1,128)S(1)}, f32[1,320]{1,0:T(1,128)S(1)}, u32[]{:S(2)}, u32[]{:S(2)}) collective-permute-start(f32[1,320]{1,0:T(1,128)S(1)} %get-tuple-element.200), channel_id=1, source_target_pairs={{1,0},{2,1},{3,2},{4,3},{5,4},{6,5},{7,6},{9,8},{10,9},{11,10},{12... | collective-permute-start | bytes 3848 | tf_op jit(solution)/shard_map/ppermute | solution.py:177
  30.6 4.9 %collective-permute-start.3 = (f32[16,384]{1,0:T(8,128)S(1)}, f32[16,384]{1,0:T(8,128)S(1)}, u32[]{:S(2)}, u32[]{:S(2)}) collective-permute-start(f32[16,384]{1,0:T(8,128)S(1)} %get-tuple-element.105), channel_id=1, source_target_pairs={{0,8},{1,9},{2,10},{3,11},{4,12},{5,13},{6,14},{7,15}} | collective-permute-start | bytes 73736 | tf_op jit(solution)/shard_map/ppermute | solution.py:197
  37.4 5.9 %collective-permute-start.4 = (f32[16,384]{1,0:T(8,128)S(1)}, f32[16,384]{1,0:T(8,128)S(1)}, u32[]{:S(2)}, u32[]{:S(2)}) collective-permute-start(f32[16,384]{1,0:T(8,128)S(1)} %get-tuple-element.107), channel_id=1, source_target_pairs={{0,8},{8,16},{1,9},{9,17},{2,10},{10,18},{3,11},{11,19},{4,12},{12... | collective-permute-start | bytes 73736 | tf_op jit(solution)/shard_map/ppermute | solution.py:197
  45.2 5.7 %collective-permute-start.5 = (f32[16,384]{1,0:T(8,128)S(1)}, f32[16,384]{1,0:T(8,128)S(1)}, u32[]{:S(2)}, u32[]{:S(2)}) collective-permute-start(f32[16,384]{1,0:T(8,128)S(1)} %get-tuple-element.109), channel_id=1, source_target_pairs={{0,8},{8,16},{16,24},{1,9},{9,17},{17,25},{2,10},{10,18},{18,26},{... | collective-permute-start | bytes 73736 | tf_op jit(solution)/shard_map/ppermute | solution.py:197
  52.8 5.7 %collective-permute-start.6 = (f32[16,384]{1,0:T(8,128)S(1)}, f32[16,384]{1,0:T(8,128)S(1)}, u32[]{:S(2)}, u32[]{:S(2)}) collective-permute-start(f32[16,384]{1,0:T(8,128)S(1)} %get-tuple-element.111), channel_id=1, source_target_pairs={{0,8},{8,16},{16,24},{24,32},{1,9},{9,17},{17,25},{25,33},{2,10},{... | collective-permute-start | bytes 73736 | tf_op jit(solution)/shard_map/ppermute | solution.py:197
  59.1 0.7 collective-permute-start.7
  60.3 0.7 collective-permute-start.8
  61.6 0.7 collective-permute-start.9
  62.8 0.7 collective-permute-start.10
  64.1 0.7 collective-permute-start.11
  65.3 0.7 collective-permute-start.12
  66.5 0.7 collective-permute-start.13
  67.8 0.7 collective-permute-start.14
  69.0 0.7 collective-permute-start.15
  70.3 0.7 collective-permute-start.16
  71.7 69.8 %collective-permute-start.17 = (f32[16,384]{1,0:T(8,128)S(1)}, f32[16,384]{1,0:T(8,128)S(1)}, u32[]{:S(2)}, u32[]{:S(2)}) collective-permute-start(f32[16,384]{1,0:T(8,128)S(1)} %get-tuple-element.133), channel_id=1, source_target_pairs={{88,96},{96,104},{104,112},{112,120},{89,97},{97,105},{105,113},{1... | collective-permute-start | bytes 73736 | tf_op jit(solution)/shard_map/ppermute | solution.py:197
  142.0 0.7 collective-permute-start.18
  143.3 0.7 collective-permute-start.19
  144.5 0.7 collective-permute-start.20
  147.9 5.6 %collective-permute-start.21 = (f32[1,320]{1,0:T(1,128)S(1)}, f32[1,320]{1,0:T(1,128)S(1)}, u32[]{:S(2)}, u32[]{:S(2)}) collective-permute-start(f32[1,320]{1,0:T(1,128)S(1)} %get-tuple-element.199), channel_id=1, source_target_pairs={{0,1},{1,2},{2,3},{3,4},{4,5},{5,6},{6,7},{8,9},{9,10},{10,11},{11... | collective-permute-start | bytes 3848 | tf_op jit(solution)/shard_map/ppermute | solution.py:177
  149.9 4.8 %collective-permute-start.22 = (f32[1,320]{1,0:T(1,128)S(1)}, f32[1,320]{1,0:T(1,128)S(1)}, u32[]{:S(2)}, u32[]{:S(2)}) collective-permute-start(f32[1,320]{1,0:T(1,128)S(1)} %get-tuple-element.198), channel_id=1, source_target_pairs={{1,0},{2,1},{3,2},{4,3},{5,4},{6,5},{7,6},{9,8},{10,9},{11,10},{12... | collective-permute-start | bytes 3848 | tf_op jit(solution)/shard_map/ppermute | solution.py:177
  156.6 0.7 collective-permute-start.23
  158.4 0.7 collective-permute-start.24
  160.2 0.7 collective-permute-start.25
  162.0 51.8 %collective-permute-start.26 = (f32[16,384]{1,0:T(8,128)S(1)}, f32[16,384]{1,0:T(8,128)S(1)}, u32[]{:S(2)}, u32[]{:S(2)}) collective-permute-start(f32[16,384]{1,0:T(8,128)S(1)} %get-tuple-element.168), channel_id=1, source_target_pairs={{120,112},{112,104},{104,96},{96,88},{121,113},{113,105},{105,97},... | collective-permute-start | bytes 73736 | tf_op jit(solution)/shard_map/ppermute | solution.py:197
  226.0 0.9 collective-permute-start.33
  233.5 67.8 %collective-permute-start.37 = (f32[16,384]{1,0:T(8,128)S(1)}, f32[16,384]{1,0:T(8,128)S(1)}, u32[]{:S(2)}, u32[]{:S(2)}) collective-permute-start(f32[16,384]{1,0:T(8,128)S(1)} %get-tuple-element.190), channel_id=1, source_target_pairs={{32,24},{24,16},{16,8},{8,0},{33,25},{25,17},{17,9},{9,1},{34,26},... | collective-permute-start | bytes 73736 | tf_op jit(solution)/shard_map/ppermute | solution.py:197
  303.9 7.6 %collective-permute-start.38 = (f32[16,384]{1,0:T(8,128)S(1)}, f32[16,384]{1,0:T(8,128)S(1)}, u32[]{:S(2)}, u32[]{:S(2)}) collective-permute-start(f32[16,384]{1,0:T(8,128)S(1)} %get-tuple-element.192), channel_id=1, source_target_pairs={{24,16},{16,8},{8,0},{25,17},{17,9},{9,1},{26,18},{18,10},{10,2},{... | collective-permute-start | bytes 73736 | tf_op jit(solution)/shard_map/ppermute | solution.py:197
  314.0 7.8 %collective-permute-start.39 = (f32[16,384]{1,0:T(8,128)S(1)}, f32[16,384]{1,0:T(8,128)S(1)}, u32[]{:S(2)}, u32[]{:S(2)}) collective-permute-start(f32[16,384]{1,0:T(8,128)S(1)} %get-tuple-element.194), channel_id=1, source_target_pairs={{16,8},{8,0},{17,9},{9,1},{18,10},{10,2},{19,11},{11,3},{20,12},{1... | collective-permute-start | bytes 73736 | tf_op jit(solution)/shard_map/ppermute | solution.py:197
  324.4 5.9 %collective-permute-start.40 = (f32[16,384]{1,0:T(8,128)S(1)}, f32[16,384]{1,0:T(8,128)S(1)}, u32[]{:S(2)}, u32[]{:S(2)}) collective-permute-start(f32[16,384]{1,0:T(8,128)S(1)} %get-tuple-element.196), channel_id=1, source_target_pairs={{8,0},{9,1},{10,2},{11,3},{12,4},{13,5},{14,6},{15,7}} | collective-permute-start | bytes 73736 | tf_op jit(solution)/shard_map/ppermute | solution.py:197
  (14 other events, 30.2 us)

commit v2 on v1

v2 whole, which is shorter than its diff:
```python
import functools

import jax
import jax.numpy as jnp
from jax import lax
from jax.experimental import pallas as pl
from jax.experimental.pallas import tpu as pltpu
from jax.sharding import PartitionSpec as P

GROUPS = 2
BLOCK = 8
NVAR = 5
NB = 64
WIDE = 384
ORDER = (0, 1)
STEP_VMEM = 3 << 20
PREP_VMEM = 24 << 20

VMEM_SPEC = pl.BlockSpec(memory_space=pltpu.VMEM)
ANY_SPEC = pl.BlockSpec(memory_space=pl.ANY)
F32 = jnp.float32
BF16 = jnp.bfloat16


def dot(a, b):
    return jnp.dot(a, b, preferred_element_type=jnp.float32)


def split(x):
    high = x.astype(jnp.bfloat16)
    low = (x - high.astype(jnp.float32)).astype(jnp.bfloat16)
    return high, low


def couple(x, lift_high, lift_low, mix):
    m = x.shape[0]
    stacked = jnp.concatenate([x[:, :128], x[:, 128:256], x[:, 256:]], axis=0)
    high, low = split(stacked)
    spread = dot(jnp.concatenate([high, low], axis=1), lift_high) + dot(high, lift_low)
    parts = [spread[v // 2 * m : v // 2 * m + m, v % 2 * 128 : v % 2 * 128 + 128] for v in range(NVAR)]
    chunks = []
    for k in range(3):
        at = slice(128 * k, 128 * k + 128)
        total = mix[0][:, at] * parts[0]
        for v in range(1, NVAR):
            total = total + mix[v][:, at] * parts[v]
        chunks.append(total)
    return jnp.concatenate(chunks, axis=1)


def padded(x):
    return jnp.concatenate([x, jnp.zeros((x.shape[0], WIDE - x.shape[1]), x.dtype)], axis=1)


def dot_t(a, b):
    return lax.dot_general(a, b, (((1,), (1,)), ((), ())), preferred_element_type=F32)


def gathered(x, delta):
    rows = x.shape[0]
    cells = x.reshape(rows // 8, 8, x.shape[1])
    chunks = []
    for k in range(3):
        chunk = cells[:, :, 128 * k : 128 * k + 128]
        moved = chunk
        for d in (-3, -2, -1, 1, 2, 3):
            moved = jnp.where(delta.reshape(rows // 8, 8, 128) == d, pltpu.roll(chunk, (-d) % 8, 1), moved)
        chunks.append(moved.reshape(rows, 128))
    return jnp.concatenate(chunks, axis=1)


def load_kernel(
    inverse_ref, flux_ref, lift_ref,
    main_ref, rem_ref, mix_ref, high_ref, low_ref, tail_ref, main_sem, tail_sem,
):
    elems = tail_ref.shape[0]
    tail_copy = pltpu.make_async_copy(inverse_ref.at[:, :, pl.ds(256, 64)], tail_ref, tail_sem)
    main_copy = pltpu.make_async_copy(inverse_ref.at[:, :, pl.ds(0, 256)], main_ref, main_sem)
    tail_copy.start()
    main_copy.start()
    lane = lax.broadcasted_iota(jnp.int32, (elems, 128), 1)
    for d in range(4):
        lift_t = lift_ref[d].T
        both = jnp.concatenate([lift_t, lift_t], axis=1)
        none = jnp.zeros_like(both)
        weight = jnp.concatenate(
            [jnp.concatenate([both, none], axis=1), jnp.concatenate([none, both], axis=1)], axis=0
        )
        high, low = split(weight)
        high_ref[d] = jnp.concatenate([high, high], axis=0)
        low_ref[d] = low
        flux = flux_ref[d]
        for v in range(NVAR):
            for k in range(3):
                u = 2 * k
                first = jnp.broadcast_to(flux[:, 5 * u + v : 5 * u + v + 1], (elems, 128))
                if u + 1 < NVAR:
                    at = 5 * (u + 1) + v
                    second = jnp.broadcast_to(flux[:, at : at + 1], (elems, 128))
                else:
                    second = jnp.zeros((elems, 128), F32)
                mix_ref[d, v, :, 128 * k : 128 * k + 128] = jnp.where(lane < NB, first, second)
    tail_copy.wait()

    @pl.loop(0, elems // 4)
    def _(q):
        rem_ref[q] = jnp.concatenate([tail_ref[4 * q + j] for j in range(4)], axis=1)

    main_copy.wait()


def face_of(x, d, mix_ref, high_ref, low_ref):
    return couple(x, high_ref[d], low_ref[d], [mix_ref[d, v] for v in range(NVAR)])


def beside(shift_ref, left_ref, right_ref):
    elems = shift_ref.shape[0] - 16
    shift_ref[7:8, :] = left_ref[...]
    shift_ref[elems + 8 : elems + 9, :] = right_ref[...]
    return shift_ref[7 : elems + 7, :], shift_ref[9 : elems + 9, :]


def put_groups(fixed, refs):
    width = refs[0].shape[0]
    for p, ref in enumerate(refs):
        ref[...] = fixed[p * width : p * width + width]


def setup_kernel(
    rhs_ref, old_ref, next_ref, left_ref, right_ref, delta_ref, mix_ref, high_ref, low_ref, *refs
):
    fixed_refs, (source_ref, shift_ref) = refs[:GROUPS], refs[GROUPS:]
    elems = rhs_ref.shape[0]
    source = padded(rhs_ref[...])
    source_ref[...] = source
    shift_ref[8 : elems + 8, :] = padded(old_ref[...])
    before, after = beside(shift_ref, left_ref, right_ref)
    below = gathered(padded(next_ref[...]), delta_ref[...])
    fixed = source - face_of(below, 1, mix_ref, high_ref, low_ref)
    fixed = fixed - face_of(before, 2, mix_ref, high_ref, low_ref)
    put_groups(fixed - face_of(after, 3, mix_ref, high_ref, low_ref), fixed_refs)


def turn_kernel(source_ref, left_ref, right_ref, mix_ref, high_ref, low_ref, *refs):
    states, uppers = refs[:GROUPS], refs[GROUPS : 2 * GROUPS]
    fixed_refs, (half_ref, shift_ref) = refs[2 * GROUPS : 3 * GROUPS], refs[3 * GROUPS :]
    width = states[0].shape[0]
    for p in range(GROUPS):
        shift_ref[8 + p * width : 8 + p * width + width, :] = states[p][...]
        half_ref[p * width : p * width + width, :] = states[p][:, :320]
    before, after = beside(shift_ref, left_ref, right_ref)
    fixed = source_ref[...] - jnp.concatenate([upper[...] for upper in uppers], axis=0)
    fixed = fixed - face_of(before, 2, mix_ref, high_ref, low_ref)
    put_groups(fixed - face_of(after, 3, mix_ref, high_ref, low_ref), fixed_refs)


def join_kernel(*refs):
    width = refs[0].shape[0]
    for p in range(GROUPS):
        refs[GROUPS][p * width : p * width + width, :] = refs[p][:, :320]


def step_kernel(
    layer, face, group, keep,
    message_ref, main_ref, rem_ref, fixed_ref, mix_ref, high_ref, low_ref, delta_ref, live_ref,
    token_ref, *refs,
):
    del token_ref
    count = 2 if keep else 1
    held_refs, (out_ref, *new_refs, body_ref) = refs[:count], refs[count:]
    width = message_ref.shape[0]
    active = lax.axis_index("flow") == layer

    @pl.when(active)
    def _():
        base = group * width
        rows = pl.ds(base, width)
        mix = [mix_ref[face, v, rows, :] for v in range(NVAR)]
        inflow = couple(gathered(message_ref[...], delta_ref[rows, :]), high_ref[face], low_ref[face], mix)
        if keep:
            new_refs[1][...] = inflow
        resid = fixed_ref[...] - inflow
        tail = resid[:, 256:]
        tail = tail + pltpu.roll(tail, 64, 1)
        row = lax.broadcasted_iota(jnp.int32, (width, 256), 0)
        lane = lax.broadcasted_iota(jnp.int32, (width, 256), 1)
        body_ref[:, :256] = resid[:, :256]
        body_ref[:, 256:] = jnp.where(row % 4 == lane // 64, jnp.concatenate([tail, tail], axis=1), 0.0)
        at = lax.broadcasted_iota(jnp.int32, (BLOCK, 320), 0)

        @pl.loop(0, width // BLOCK)
        def _(b):
            part = pl.ds(pl.multiple_of(b * BLOCK, BLOCK), BLOCK)
            both = body_ref[part, :].astype(BF16)
            first = base + b * BLOCK
            rest = jnp.zeros((BLOCK, 320), F32)
            solved = jnp.zeros((BLOCK, 320), F32)
            for q in range(BLOCK // 4):
                rest = jnp.where(at // 4 == q, dot_t(both[:, 256:], rem_ref[first // 4 + q]), rest)
                for e in range(4 * q, 4 * q + 4):
                    solved = jnp.where(at == e, dot_t(both[:, :256], main_ref[first + e]), solved)
            wide = padded(solved + rest)
            live = live_ref[pl.ds(pl.multiple_of(first, BLOCK), BLOCK), :]
            wide = wide * jnp.concatenate([live, live, live], axis=1)
            new_refs[0][part, :] = wide
            out_ref[part, :] = wide

    @pl.when(jnp.logical_not(active))
    def _():
        for held, new in zip(held_refs, new_refs):
            new[...] = held[...]


def step_call(layer, face, group, keep, width):
    body = functools.partial(step_kernel, layer, face, group, keep)
    count = 2 if keep else 1
    cells = jax.ShapeDtypeStruct((width, WIDE), F32)
    return pl.pallas_call(
        body,
        out_shape=(cells,) * (1 + count),
        in_specs=[VMEM_SPEC] * 9 + [ANY_SPEC] + [VMEM_SPEC] * count,
        out_specs=(VMEM_SPEC,) * (1 + count),
        scratch_shapes=[pltpu.VMEM((width, 512), F32)],
        compiler_params=pltpu.CompilerParams(vmem_limit_bytes=STEP_VMEM),
        cost_estimate=pl.CostEstimate(flops=width * 320 * 320 * 2, bytes_accessed=width * 320 * 320 * 2, transcendentals=0),
        name="sweep_step",
    )


def edge_rows(first, last):
    count = lax.axis_size("cross")
    right = [(i, i + 1) for i in range(count - 1)]
    left = [(i + 1, i) for i in range(count - 1)]
    return lax.ppermute(last, "cross", right), lax.ppermute(first, "cross", left)


def sweep(fixed, table, delta, live, face, keep, route):
    width = fixed[0].shape[0]
    blank = jnp.zeros((width, WIDE), F32)
    messages = [blank] * GROUPS
    held = [(blank,) * (2 if keep else 1)] * GROUPS
    token = fixed[0]
    last = len(route) - 1
    for i, layer in enumerate(route):
        for p in ORDER:
            call = step_call(layer, face, p, keep, width)
            main, rem, mix, high, low = table
            out, *new = call(
                messages[p], main, rem, fixed[p], mix, high, low, delta, live, token, *held[p]
            )
            token = out
            held[p] = tuple(new)
            if i < last:
                messages[p] = lax.ppermute(out, "flow", [(i, i + 1), (last - i, last - i - 1)])
    return held


def per_device(
    right_side, old_state, block_inverse, flux_jacobian, face_lift, upstream, downstream, live_counts
):
    layers = lax.axis_size("flow")
    rhs = right_side[0]
    elems = rhs.shape[0]
    width = elems // GROUPS
    slot = jnp.arange(elems, dtype=jnp.int32)[:, None]
    up = jnp.broadcast_to(upstream[0][:, None] % elems - slot, (elems, 128))
    down = jnp.broadcast_to(downstream[0][:, None] % elems - slot, (elems, 128))
    live = jnp.broadcast_to((slot < live_counts[0, 0]).astype(F32), (elems, 128))
    old = jnp.where(slot < live_counts[0, 0], old_state[0], 0.0)
    following = lax.ppermute(old, "flow", [(l + 1, l) for l in range(layers - 1)])
    edge = jnp.pad(old[:1], ((0, 0), (0, WIDE - 320))), jnp.pad(old[-1:], ((0, 0), (0, WIDE - 320)))
    left, right = edge_rows(*edge)
    flux = jnp.transpose(flux_jacobian[0], (1, 0, 2))
    shift = pltpu.VMEM((elems + 16, WIDE), F32)
    cells = jax.ShapeDtypeStruct((elems, WIDE), F32)
    group_cells = (jax.ShapeDtypeStruct((width, WIDE), F32),) * GROUPS
    prep = pltpu.CompilerParams(vmem_limit_bytes=PREP_VMEM)
    table = pl.pallas_call(
        load_kernel,
        out_shape=(
            jax.ShapeDtypeStruct((elems, 320, 256), BF16),
            jax.ShapeDtypeStruct((elems // 4, 320, 256), BF16),
            jax.ShapeDtypeStruct((4, NVAR, elems, WIDE), F32),
            jax.ShapeDtypeStruct((4, 256, 256), BF16),
            jax.ShapeDtypeStruct((4, 128, 256), BF16),
        ),
        in_specs=[ANY_SPEC] + [VMEM_SPEC] * 2,
        out_specs=(VMEM_SPEC,) * 5,
        scratch_shapes=[
            pltpu.VMEM((elems, 320, 64), BF16), pltpu.SemaphoreType.DMA, pltpu.SemaphoreType.DMA
        ],
        compiler_params=prep,
        name="sweep_load",
    )(block_inverse[0], flux, face_lift)
    mixing = table[2:]
    *fixed, source = pl.pallas_call(
        setup_kernel,
        out_shape=group_cells + (cells,),
        in_specs=[VMEM_SPEC] * 9,
        out_specs=(VMEM_SPEC,) * (GROUPS + 1),
        scratch_shapes=[shift],
        compiler_params=prep,
        name="sweep_setup",
    )(rhs, old, following, left, right, down, *mixing)
    held = sweep(fixed, table, up, live, 0, True, list(range(layers)))
    states = [state for state, _ in held]
    uppers = [upper for _, upper in held]
    left, right = edge_rows(states[0][:1], states[-1][-1:])
    *fixed, half = pl.pallas_call(
        turn_kernel,
        out_shape=group_cells + (jax.ShapeDtypeStruct((elems, 320), F32),),
        in_specs=[VMEM_SPEC] * (6 + 2 * GROUPS),
        out_specs=(VMEM_SPEC,) * (GROUPS + 1),
        scratch_shapes=[shift],
        compiler_params=prep,
        name="sweep_turn",
    )(source, left, right, *mixing, *states, *uppers)
    held = sweep(fixed, table, down, live, 1, False, list(reversed(range(layers))))
    full = pl.pallas_call(
        join_kernel,
        out_shape=jax.ShapeDtypeStruct((elems, 320), F32),
        in_specs=[VMEM_SPEC] * GROUPS,
        out_specs=VMEM_SPEC,
        compiler_params=pltpu.CompilerParams(vmem_limit_bytes=STEP_VMEM),
        name="sweep_join",
    )(*[state for state, in held])
    return half[None], full[None]


def solution(mesh):
    in_specs = (
        P("flow", "cross", None),
        P("flow", "cross", None),
        P("flow", "cross", None, None),
        P("flow", "cross", None, None),
        P(),
        P("flow", "cross"),
        P("flow", "cross"),
        P("flow", "cross"),
    )
    out_specs = (P("flow", "cross", None), P("flow", "cross", None))
    return jax.shard_map(
        per_device, mesh=mesh, in_specs=in_specs, out_specs=out_specs, check_vma=False
    )
```

time: 335 us -> 261 us (0.78)
  starting transfers between devices: 181 us -> 58.3 us
  waiting for transfers between devices: 91.5 us -> 173 us
  Pallas kernels: 48 us -> 20.9 us
  local copies, waits for them, and re-layouts: 8.91 us -> 2.06 us
    ppermute x40 -> x64, starting transfers between devices: 171 us -> 57.1 us  [the longest x60 45.9 us: sweep(): lax.ppermute(out, 'flow', [(i, i + 1), (last - i, last - i - 1)])]
    ppermute x40 -> x64, waiting for transfers between devices: 91.5 us -> 173 us  [the longest x60 172 us: sweep(): lax.ppermute(out, 'flow', [(i, i + 1), (last - i, last - i - 1)])]
    pallas_call x42 -> x68, Pallas kernels: 48 us -> 20.9 us  [the longest x64 12.8 us: sweep(): call(messages[p], main, rem, fixed[p], mix, high, low, delta, live, token...]
    ppermute x1, starting transfers between devices: 10.1 us -> 1.29 us  [per_device(): lax.ppermute(old, 'flow', [(l + 1, l) for l in range(layers - 1)])]
    unnamed x11 -> x5, local copies, waits for them, and re-layouts: 8.18 us -> 1.81 us
  transfers between devices with their start and end apart: 41 -> 65, of which waited for: 9 -> 8; matrix products, arithmetic and copies ran while one was open for 0% -> 1% of each run, Pallas kernels for 0% -> 5%
where the time goes in v2:
time: 261 us; the launch traced here: 259 us
  waiting for transfers between devices  173 us (66%)
  starting transfers between devices  58.3 us (22%)
  Pallas kernels  20.9 us (8%)
  between operations  2.8 us (1%)
    ppermute x60, waiting for transfers between devices, sweep(): lax.ppermute(out, 'flow', [(i, i + 1), (last - i, last - i - 1)])  172 us
    ppermute x60, starting transfers between devices, sweep(): lax.ppermute(out, 'flow', [(i, i + 1), (last - i, last - i - 1)])  45.9 us
    pallas_call x64, Pallas kernels, sweep(): call(messages[p], main, rem, fixed[p], mix, high, low, delta, live, token...  12.8 us
    ppermute x2, starting transfers between devices, edge_rows(): lax.ppermute(first, 'cross', left)  7.28 us
    pallas_call x1, Pallas kernels, per_device(): pl.pallas_call(load_kernel, out_shape=(jax.ShapeDtypeStruct((elems, 320,...  6.27 us
  transfers between devices with their start and end apart: 65, of which 8 were waited for; matrix products, arithmetic and copies ran while one was open for 1% of the time, Pallas kernels for 5%

profile of v2, /device:TPU:16, one launch (start us, length us, event | category | flops | bytes accessed | tf_op | source)
XLA Modules:
  0.0 259.5 jit_solution(970647534177865499)
XLA Ops:
  1.3 1.0 bitcast_select_fusion.old_ref
  2.3 1.3 collective-permute-start
  3.6 1.9 collective-permute-start.1
  5.6 3.6 %collective-permute-start.2 = (f32[1,384]{1,0:T(1,128)S(1)}, f32[1,384]{1,0:T(1,128)S(1)}, u32[]{:S(2)}, u32[]{:S(2)}) collective-permute-start(f32[1,384]{1,0:T(1,128)S(1)} %pad.8), channel_id=1, source_target_pairs={{1,0},{2,1},{3,2},{4,3},{5,4},{6,5},{7,6},{9,8},{10,9},{11,10},{12... | collective-permute-start | bytes 4616 | tf_op jit(solution)/shard_map/ppermute | solution.py:234
  9.2 0.7 fusion
  10.6 0.9 copy.10
  11.5 0.9 copy-done
  12.4 6.3 %sweep_load.1 = (bf16[64,320,256]{2,1,0:T(8,128)(2,1)S(1)}, bf16[16,320,256]{2,1,0:T(8,128)(2,1)S(1)}, f32[4,5,64,384]{3,2,1,0:T(8,128)S(1)}, bf16[4,256,256]{2,1,0:T(8,128)(2,1)S(1)}, bf16[4,128,256]{2,1,0:T(8,128)(2,1)S(1)}) custom-call(bf16[64,320,320]{2,1,0:T(8,128)(2,1)} %bitcast.18, f32[4,64,25]{2,1,0:T(8,128)S(1)} %bitcast.16, f32[4,64,64]{2,1,0:T(8,128)S(1)} %copy-done), custom_call_target="tpu_custom_call" | custom-call | tf_op jit(solution)/shard_map/sweep_load/pallas_call | solution.py:278
  19.3 2.4 sweep_step.64
  21.7 2.1 collective-permute-start.4
  23.8 2.4 sweep_step.65
  26.3 1.3 collective-permute-start.3
  27.6 0.7 collective-permute-start.6
  28.3 1.0 collective-permute-done.3.message_ref
  32.2 0.7 collective-permute-start.9
  47.4 1.3 collective-permute-start.32
  48.8 1.3 collective-permute-start.31
  50.1 61.3 %collective-permute-done.32.message_ref = f32[32,384]{1,0:T(8,128)S(1)} collective-permute-done((f32[32,384]{1,0:T(8,128)S(1)}, f32[32,384]{1,0:T(8,128)S(1)}, u32[]{:S(2)}, u32[]{:S(2)}) %collective-permute-start.32) | collective-permute-done | bytes 49184 | tf_op jit(solution)/shard_map/ppermute | solution.py:254
  111.4 4.4 %collective-permute-done.31.message_ref = f32[32,384]{1,0:T(8,128)S(1)} collective-permute-done((f32[32,384]{1,0:T(8,128)S(1)}, f32[32,384]{1,0:T(8,128)S(1)}, u32[]{:S(2)}, u32[]{:S(2)}) %collective-permute-start.31) | collective-permute-done | bytes 49184 | tf_op jit(solution)/shard_map/ppermute | solution.py:254
  116.4 1.9 collective-permute-start.33
  118.3 3.6 %collective-permute-start.34 = (f32[1,384]{1,0:T(1,128)S(1)}, f32[1,384]{1,0:T(1,128)S(1)}, u32[]{:S(2)}, u32[]{:S(2)}) collective-permute-start(f32[1,384]{1,0:T(1,128)S(1)} %slice.15), channel_id=1, source_target_pairs={{1,0},{2,1},{3,2},{4,3},{5,4},{6,5},{7,6},{9,8},{10,9},{11,10},{12... | collective-permute-start | bytes 4616 | tf_op jit(solution)/shard_map/ppermute | solution.py:234
  122.0 1.3 collective-permute-done.34.right_ref
  123.2 0.9 sweep_turn.1
  124.1 1.6 collective-permute-start.35
  125.7 1.3 collective-permute-start.37
  128.1 0.7 collective-permute-done.37.message_ref
  146.8 1.3 collective-permute-start.62
  148.2 1.3 collective-permute-start.64
  149.5 102.6 %collective-permute-done.62.message_ref = f32[32,384]{1,0:T(8,128)S(1)} collective-permute-done((f32[32,384]{1,0:T(8,128)S(1)}, f32[32,384]{1,0:T(8,128)S(1)}, u32[]{:S(2)}, u32[]{:S(2)}) %collective-permute-start.62) | collective-permute-done | bytes 49184 | tf_op jit(solution)/shard_map/ppermute | solution.py:254
  252.0 2.4 sweep_step.126
  254.4 1.3 collective-permute-done.64.message_ref
  255.8 3.1 %sweep_step.127 = (f32[32,384]{1,0:T(8,128)}, f32[32,384]{1,0:T(8,128)S(1)}) custom-call(f32[32,384]{1,0:T(8,128)S(1)} %collective-permute-done.64.message_ref, bf16[64,320,256]{2,1,0:T(8,128)(2,1)S(1)} %get-tuple-element.175.main_ref, bf16[16,320,256]{2,1,0:T(8,128)(2,1)S(1)} %get-tuple-element.176.rem_ref, f32[32,384]{1,0:T(8,128)S(1)} %get-tuple-element.277.fixed_ref, ...), custom_call_target="tpu_custom_call" | custom-call | flops 6553600 | bytes 6553600 | tf_op jit(solution)/shard_map/sweep_step/pallas_call | solution.py:248
  (185 shorter events, 38.0 us)
Async XLA Ops:
  2.3 16.4 %collective-permute-start = (f32[64,320]{1,0:T(8,128)S(1)}, f32[64,320]{1,0:T(8,128)S(1)}, u32[]{:S(2)}, u32[]{:S(2)}) collective-permute-start(f32[64,320]{1,0:T(8,128)S(1)} %bitcast_select_fusion.old_ref), channel_id=1, source_target_pairs={{8,0},{16,8},{24,16},{32,24},{40,32},{48,40},{56,48},{64,56},{72,6... | collective-permute-start | bytes 245768 | tf_op jit(solution)/shard_map/ppermute | solution.py:270
  3.6 15.0 %collective-permute-start.1 = (f32[1,384]{1,0:T(1,128)S(1)}, f32[1,384]{1,0:T(1,128)S(1)}, u32[]{:S(2)}, u32[]{:S(2)}) collective-permute-start(f32[1,384]{1,0:T(1,128)S(1)} %pad.7), channel_id=1, source_target_pairs={{0,1},{1,2},{2,3},{3,4},{4,5},{5,6},{6,7},{8,9},{9,10},{10,11},{11... | collective-permute-start | bytes 4616 | tf_op jit(solution)/shard_map/ppermute | solution.py:234
  5.6 13.1 %collective-permute-start.2 = (f32[1,384]{1,0:T(1,128)S(1)}, f32[1,384]{1,0:T(1,128)S(1)}, u32[]{:S(2)}, u32[]{:S(2)}) collective-permute-start(f32[1,384]{1,0:T(1,128)S(1)} %pad.8), channel_id=1, source_target_pairs={{1,0},{2,1},{3,2},{4,3},{5,4},{6,5},{7,6},{9,8},{10,9},{11,10},{12... | collective-permute-start | bytes 4616 | tf_op jit(solution)/shard_map/ppermute | solution.py:234
  21.7 5.9 %collective-permute-start.4 = (f32[32,384]{1,0:T(8,128)S(1)}, f32[32,384]{1,0:T(8,128)S(1)}, u32[]{:S(2)}, u32[]{:S(2)}) collective-permute-start(f32[32,384]{1,0:T(8,128)S(1)} %get-tuple-element.179.token_ref), channel_id=1, source_target_pairs={{0,8},{120,112},{1,9},{121,113},{2,10},{122,114},{3,11},{123,115},... | collective-permute-start | bytes 147464 | tf_op jit(solution)/shard_map/ppermute | solution.py:254
  26.3 3.0 %collective-permute-start.3 = (f32[32,384]{1,0:T(8,128)S(1)}, f32[32,384]{1,0:T(8,128)S(1)}, u32[]{:S(2)}, u32[]{:S(2)}) collective-permute-start(f32[32,384]{1,0:T(8,128)S(1)} %get-tuple-element.180.token_ref), channel_id=1, source_target_pairs={{0,8},{120,112},{1,9},{121,113},{2,10},{122,114},{3,11},{123,115},... | collective-permute-start | bytes 147464 | tf_op jit(solution)/shard_map/ppermute | solution.py:254
  27.6 2.4 collective-permute-start.6
  30.0 1.4 collective-permute-start.8
  30.8 1.4 collective-permute-start.7
  31.5 1.4 collective-permute-start.10
  32.2 1.4 collective-permute-start.9
  32.9 1.4 collective-permute-start.12
  36.5 1.4 collective-permute-start.15
  37.2 1.4 collective-permute-start.18
  37.9 1.4 collective-permute-start.17
  38.6 1.4 collective-permute-start.20
  39.4 1.4 collective-permute-start.19
  40.1 1.4 collective-permute-start.22
  42.9 1.4 collective-permute-start.26
  43.7 1.6 collective-permute-start.25
  44.6 1.4 collective-permute-start.28
  46.7 2.0 collective-permute-start.29
  47.4 63.9 %collective-permute-start.32 = (f32[32,384]{1,0:T(8,128)S(1)}, f32[32,384]{1,0:T(8,128)S(1)}, u32[]{:S(2)}, u32[]{:S(2)}) collective-permute-start(f32[32,384]{1,0:T(8,128)S(1)} %get-tuple-element.261.token_ref), channel_id=1, source_target_pairs={{112,120},{8,0},{113,121},{9,1},{114,122},{10,2},{115,123},{11,3},... | collective-permute-start | bytes 147464 | tf_op jit(solution)/shard_map/ppermute | solution.py:254
  48.8 67.0 %collective-permute-start.31 = (f32[32,384]{1,0:T(8,128)S(1)}, f32[32,384]{1,0:T(8,128)S(1)}, u32[]{:S(2)}, u32[]{:S(2)}) collective-permute-start(f32[32,384]{1,0:T(8,128)S(1)} %get-tuple-element.264.token_ref), channel_id=1, source_target_pairs={{112,120},{8,0},{113,121},{9,1},{114,122},{10,2},{115,123},{11,3},... | collective-permute-start | bytes 147464 | tf_op jit(solution)/shard_map/ppermute | solution.py:254
  116.4 5.6 %collective-permute-start.33 = (f32[1,384]{1,0:T(1,128)S(1)}, f32[1,384]{1,0:T(1,128)S(1)}, u32[]{:S(2)}, u32[]{:S(2)}) collective-permute-start(f32[1,384]{1,0:T(1,128)S(1)} %slice.14), channel_id=1, source_target_pairs={{0,1},{1,2},{2,3},{3,4},{4,5},{5,6},{6,7},{8,9},{9,10},{10,11},{11... | collective-permute-start | bytes 4616 | tf_op jit(solution)/shard_map/ppermute | solution.py:234
  118.3 4.9 %collective-permute-start.34 = (f32[1,384]{1,0:T(1,128)S(1)}, f32[1,384]{1,0:T(1,128)S(1)}, u32[]{:S(2)}, u32[]{:S(2)}) collective-permute-start(f32[1,384]{1,0:T(1,128)S(1)} %slice.15), channel_id=1, source_target_pairs={{1,0},{2,1},{3,2},{4,3},{5,4},{6,5},{7,6},{9,8},{10,9},{11,10},{12... | collective-permute-start | bytes 4616 | tf_op jit(solution)/shard_map/ppermute | solution.py:234
  124.1 3.3 %collective-permute-start.35 = (f32[32,384]{1,0:T(8,128)S(1)}, f32[32,384]{1,0:T(8,128)S(1)}, u32[]{:S(2)}, u32[]{:S(2)}) collective-permute-start(f32[32,384]{1,0:T(8,128)S(1)} %get-tuple-element.276.token_ref), channel_id=1, source_target_pairs={{0,8},{120,112},{1,9},{121,113},{2,10},{122,114},{3,11},{123,115},... | collective-permute-start | bytes 147464 | tf_op jit(solution)/shard_map/ppermute | solution.py:254
  125.7 3.0 %collective-permute-start.37 = (f32[32,384]{1,0:T(8,128)S(1)}, f32[32,384]{1,0:T(8,128)S(1)}, u32[]{:S(2)}, u32[]{:S(2)}) collective-permute-start(f32[32,384]{1,0:T(8,128)S(1)} %get-tuple-element.278.token_ref), channel_id=1, source_target_pairs={{0,8},{120,112},{1,9},{121,113},{2,10},{122,114},{3,11},{123,115},... | collective-permute-start | bytes 147464 | tf_op jit(solution)/shard_map/ppermute | solution.py:254
  127.4 2.0 collective-permute-start.36
  140.2 1.6 collective-permute-start.55
  146.1 2.0 collective-permute-start.63
  146.8 105.2 %collective-permute-start.62 = (f32[32,384]{1,0:T(8,128)S(1)}, f32[32,384]{1,0:T(8,128)S(1)}, u32[]{:S(2)}, u32[]{:S(2)}) collective-permute-start(f32[32,384]{1,0:T(8,128)S(1)} %get-tuple-element.332.token_ref), channel_id=1, source_target_pairs={{112,120},{8,0},{113,121},{9,1},{114,122},{10,2},{115,123},{11,3},... | collective-permute-start | bytes 147464 | tf_op jit(solution)/shard_map/ppermute | solution.py:254
  148.2 107.6 %collective-permute-start.64 = (f32[32,384]{1,0:T(8,128)S(1)}, f32[32,384]{1,0:T(8,128)S(1)}, u32[]{:S(2)}, u32[]{:S(2)}) collective-permute-start(f32[32,384]{1,0:T(8,128)S(1)} %get-tuple-element.334.token_ref), channel_id=1, source_target_pairs={{112,120},{8,0},{113,121},{9,1},{114,122},{10,2},{115,123},{11,3},... | collective-permute-start | bytes 147464 | tf_op jit(solution)/shard_map/ppermute | solution.py:254
  (35 other events, 64.9 us)
